TPU v7x, 128 devices: a whole 4x4x4 slice. The times are simulated.
128 devices in a mesh: gx: 8 (over y, core), gy: 16 (over x, z).
Axes of the slice: x: 4, y: 4, z: 4, core: 2. Of those that a mesh axis runs over, the one named last changes fastest.
Arguments:
- cotangent: float32 [6, 8, 1024, 1024], P(None, None, 'gy', 'gx'), may hold values from -6 to 6
- permeability: float32 [6, 1024, 1024], P(None, 'gy', 'gx'), may hold values from 0.2 to 5
- well_mask: int32 [1024, 1024], P('gy', 'gx'), may hold values 0 or 1
- diag_block: bfloat16 [6, 8, 8, 1024, 1024], P(None, None, None, 'gy', 'gx'), may hold values from -2 to 2
- flux_block: bfloat16 [6, 8, 8, 1024, 1024], P(None, None, None, 'gy', 'gx'), may hold values from -0.875 to 0.875
- cell_list: int32 [16, 8, 16384], P('gy', 'gx'), may hold values from 0 to 49151, as said below
- block_count: int32 [16, 8], P('gy', 'gx'), may hold values from 64 to 128, as said below
- helper_of: int32 [16, 8, 128], P('gy', 'gx'), may hold values from 0 to 127, as said below
- flash_inverse: bfloat16 [16, 8, 128, 8, 8, 128], P('gy', 'gx'), may hold values from -2 to 2
- flash_coupling: bfloat16 [16, 8, 128, 8, 8, 128], P('gy', 'gx'), may hold values from -2 to 2
- phase_state: bfloat16 [16, 8, 128, 8, 128], P('gy', 'gx'), may hold values from 0.049804688 to 1
Outputs:
- adjoint: float32 [6, 8, 1024, 1024], P(None, None, 'gy', 'gx')
- interaction_grad: float32 [8, 8], replicated
Inputs may be any that keep to these rules, and one draw needn't show every extreme that they name: `cell_list`: within one brick the 16384 entries are distinct cells of that brick. `block_count`: some brick has 128 live blocks. `helper_of`: each brick's row is a permutation of all helpers; helper h is the device at gx index h // 16 and gy index h % 16.
All inputs are finite; a program needn't handle non-finite values. No bound on the sum of `well_mask` on one device may be relied on, other than what follows from the above.
Results may differ from a plain program's by a relative error of at most 0.0075.
Values may be sent and summed in bfloat16 or wider, within the bound.
A program may use at most 192 MiB of HBM per device.

v0:
```python
import math

import jax
import jax.numpy as jnp
from jax import lax
from jax.sharding import PartitionSpec as P

OFFSETS = ((1, 0, 0), (-1, 0, 0), (0, 1, 0), (0, -1, 0), (0, 0, 1), (0, 0, -1))


def with_halo(array, sides, width):
    for axis, dim in sides:
        count, length = (lax.axis_size(axis), array.shape[dim])
        up = [(i, (i + 1) % count) for i in range(count - 1)]
        down = [(j, i) for i, j in up]
        last = lax.slice_in_dim(array, length - width, length, axis=dim)
        first = lax.slice_in_dim(array, 0, width, axis=dim)
        before = lax.ppermute(last, axis, up)
        after = lax.ppermute(first, axis, down)
        array = jnp.concatenate([before, array, after], axis=dim)
    return array


def transmissibility(padded_perm, layers, rows_y, cols_x):
    centre = padded_perm[1 : 1 + layers, 1 : 1 + rows_y, 1 : 1 + cols_x]
    result = []
    for step_z, step_y, step_x in OFFSETS:
        beside = padded_perm[
            1 + step_z : 1 + step_z + layers,
            1 + step_y : 1 + step_y + rows_y,
            1 + step_x : 1 + step_x + cols_x,
        ]
        result.append(2.0 * centre * beside / (centre + beside))
    return result


def neighbour_sum(padded, trans_list, layers, rows_y, cols_x):
    summed = jnp.zeros((layers, padded.shape[1], rows_y, cols_x), jnp.float32)
    for weights, (step_z, step_y, step_x) in zip(trans_list, OFFSETS):
        beside = padded[
            1 + step_z : 1 + step_z + layers,
            :,
            1 + step_y : 1 + step_y + rows_y,
            1 + step_x : 1 + step_x + cols_x,
        ]
        summed = summed + weights[:, None] * beside
    return summed


def blocks_transposed(blocks, source_field):
    return jnp.sum(blocks * source_field[:, :, None], axis=1)


def flash_terms(inverse, coupling, chosen, phase_rows):
    multiplier = jnp.einsum("nrck,nrk->nck", inverse, chosen, preferred_element_type=jnp.float32)
    correction = (
        -jnp.einsum("nrck,nrk->nck", coupling, multiplier, preferred_element_type=jnp.float32)
    ).astype(jnp.bfloat16)
    state_wide = phase_rows.astype(jnp.float32)
    partial_sum = jnp.einsum("nik,njk->ij", multiplier * state_wide, state_wide)
    return (correction, partial_sum)


def shards(
    cotangent,
    permeability,
    well_mask,
    diag_block,
    flux_block,
    cell_list,
    block_count,
    helper_of,
    flash_inverse,
    flash_coupling,
    phase_state,
):
    layers, components, rows_y, cols_x = cotangent.shape
    well_field = well_mask.astype(jnp.float32)
    padded_perm = with_halo(permeability, (("gy", 1), ("gx", 2)), 1)
    padded_perm = jnp.pad(padded_perm, ((1, 1), (0, 0), (0, 0)))
    trans_list = transmissibility(padded_perm, layers, rows_y, cols_x)

    def apply_transposed(source_field):
        masked = source_field * (1.0 - well_field)
        padded = with_halo(masked, (("gy", 2), ("gx", 3)), 1)
        padded = jnp.pad(padded, ((1, 1), (0, 0), (0, 0), (0, 0)))
        summed = neighbour_sum(padded, trans_list, layers, rows_y, cols_x)
        return (
            blocks_transposed(diag_block, masked)
            - blocks_transposed(flux_block, summed)
            + well_field * source_field
        )

    first_apply = apply_transposed(cotangent)
    flat_cells = first_apply.transpose(1, 0, 2, 3).reshape(components, layers * rows_y * cols_x)
    slot_cells = cell_list.reshape(-1)
    targets = helper_of.reshape(-1)
    block_slots = targets.shape[0]
    block_size = flash_inverse.shape[-1]
    picked = (
        flat_cells[:, slot_cells].reshape(components, block_slots, block_size).transpose(1, 0, 2)
    )
    live_slots = jnp.arange(block_slots, dtype=jnp.int32) < block_count.reshape(())
    picked = jnp.where(live_slots[:, None, None], picked, 0.0).astype(jnp.bfloat16)
    inverse = flash_inverse.reshape(block_slots, components, components, block_size)
    coupling = flash_coupling.reshape(block_slots, components, components, block_size)
    phase_rows = phase_state.reshape(block_slots, components, block_size)
    width_x = lax.axis_size("gx")
    width_y = lax.axis_size("gy")
    home = (
        lax.all_to_all(inverse, ("gx", "gy"), split_axis=0, concat_axis=0, tiled=True),
        lax.all_to_all(coupling, ("gx", "gy"), split_axis=0, concat_axis=0, tiled=True),
        lax.all_to_all(phase_rows, ("gx", "gy"), split_axis=0, concat_axis=0, tiled=True),
    )
    own_terms, partial_sum = flash_terms(
        home[0][targets], home[1][targets], picked, home[2][targets]
    )
    device_count = width_x * width_y
    grad_scale = 1.0 / math.sqrt(block_size * device_count * device_count)
    interaction_grad = -grad_scale * lax.psum(partial_sum, ("gx", "gy"))
    added = (
        own_terms.transpose(1, 0, 2)
        .reshape(components, block_slots * block_size)
        .astype(jnp.float32)
    )
    flat_cells = flat_cells.at[:, slot_cells].add(added)
    second = flat_cells.reshape(components, layers, rows_y, cols_x).transpose(1, 0, 2, 3)
    adjoint = apply_transposed(second)
    return (adjoint, interaction_grad)


def solution(mesh):
    return jax.shard_map(
        shards,
        mesh=mesh,
        in_specs=(
            P(None, None, "gy", "gx"),
            P(None, "gy", "gx"),
            P("gy", "gx"),
            P(None, None, None, "gy", "gx"),
            P(None, None, None, "gy", "gx"),
            P("gy", "gx", None),
            P("gy", "gx"),
            P("gy", "gx", None),
            P("gy", "gx", None, None, None, None),
            P("gy", "gx", None, None, None, None),
            P("gy", "gx", None, None, None),
        ),
        out_specs=(P(None, None, "gy", "gx"), P()),
        check_vma=False,
    )
```

profile of v0, /device:TPU:1, one launch (start us, length us, event | category | flops | bytes accessed | tf_op | source)
XLA Modules:
  0.0 449.4 jit_solution(2321570992579450611)
XLA Ops:
  0.6 11.5 %all-to-all-start.2 = ((bf16[128,8,128]{2,1,0:T(8,128)(2,1)}), bf16[128,8,128]{2,1,0:T(8,128)(2,1)S(1)}, u32[]{:S(2)}, u32[]{:S(2)}) async-start(bf16[128,8,128]{2,1,0:T(8,128)(2,1)} %bitcast.57), calls=%async_computation.2 | async-start | bytes 524288 | tf_op jit(solution)/shard_map/all_to_all | solution.py:113
  12.9 3.4 collective-permute-start
  16.3 1.3 collective-permute-start.1
  18.4 2.5 copy_multiply_fusion
  20.9 4.0 collective-permute-start.4
  24.9 1.3 collective-permute-start.5
  26.6 3.0 fusion
  30.3 13.2 %all-to-all-start = ((bf16[128,8,8,128]{3,2,1,0:T(8,128)(2,1)}), bf16[128,8,8,128]{3,2,1,0:T(8,128)(2,1)}, u32[]{:S(2)}, u32[]{:S(2)}) async-start(bf16[128,8,8,128]{3,2,1,0:T(8,128)(2,1)} %bitcast.55), calls=%async_computation | async-start | bytes 4194304 | tf_op jit(solution)/shard_map/all_to_all | solution.py:111
  44.4 3.0 collective-permute-start.3
  47.4 2.5 collective-permute-start.2
  50.0 20.0 %collective-permute-done.3 = f32[6,66,1]{2,1,0:T(8,128)S(1)} collective-permute-done((f32[6,66,1]{2,1,0:T(8,128)S(1)}, f32[6,66,1]{2,1,0:T(8,128)S(1)}, u32[]{:S(2)}, u32[]{:S(2)}) %collective-permute-start.3) | collective-permute-done | bytes 1616 | tf_op jit(solution)/shard_map/ppermute | solution.py:19
  70.0 1.1 select_maximum_fusion.8
  72.4 1.7 fusion.37
  74.1 2.6 copy.42
  76.8 1.2 copy.41
  78.0 2.0 collective-permute-start.6
  80.0 2.9 collective-permute-start.7
  82.9 2.8 add_divide_fusion.1
  85.7 1.4 copy.44
  87.2 2.6 copy.43
  89.7 5.0 %select_maximum_fusion.4 = f32[8,8,66,130]{3,1,2,0:T(8,128)} fusion(f32[6,8,66,1]{3,1,2,0:T(8,128)S(1)} %copy.44, f32[6,8,66,1]{3,1,2,0:T(8,128)} %copy.43, f32[6,8,1,128]{3,1,2,0:T(8,128)S(1)} %copy-done.24, f32[6,8,64,128]{3,1,2,0:T(8,128)S(1)} %copy_multiply_fusion, f32[6,8,1,128]{3,1,2,0:T(8,128)S(1)} %copy-done.22), kind=kLoop, calls=%fused_computation.23 | loop fusion | flops 6589440 | bytes 3843840 | tf_op jit(solution)/shard_map/concatenate | solution.py:20
  94.8 9.8 %all-to-all-start.1 = ((bf16[128,8,8,128]{3,2,1,0:T(8,128)(2,1)}), bf16[128,8,8,128]{3,2,1,0:T(8,128)(2,1)}, u32[]{:S(2)}, u32[]{:S(2)}) async-start(bf16[128,8,8,128]{3,2,1,0:T(8,128)(2,1)} %bitcast.56), calls=%async_computation.1 | async-start | bytes 4194304 | tf_op jit(solution)/shard_map/all_to_all | solution.py:112
  104.6 5.0 %fusion.19 = f32[6,8,64,128]{3,1,2,0:T(8,128)S(1)} fusion(f32[6,8,66,1]{3,1,2,0:T(8,128)} %copy.43, f32[6,8,1,128]{3,1,2,0:T(8,128)} %copy-done.23, f32[6,8,64,128]{3,1,2,0:T(8,128)S(1)} %copy_multiply_fusion, f32[6,8,1,128]{3,1,2,0:T(8,128)} %copy-done.21, f32[6,8,66,1]{3,1,2,0:T(8,128)S(1)} %copy.44, f32[8,8,66,130]{3,1,2,0:T(8,128)} %select_maximum_fusion.4, ...), kind=kLoop, calls=%fused_computation.55 | loop fusion | flops 7471104 | bytes 7545600 | tf_op jit(solution)/shard_map/add | solution.py:46
  110.0 5.1 %fusion.2 = f32[6,8,64,128]{3,2,1,0:T(8,128)S(1)} fusion(bf16[6,8,8,64,128]{4,3,2,1,0:T(8,128)(2,1)} %param.15, f32[6,8,64,128]{3,2,1,0:T(8,128)S(1)} %copy.47), kind=kLoop, calls=%fused_computation.11 | loop fusion | flops 9043968 | bytes 9437184 | tf_op jit(solution)/shard_map/reduce_sum | solution.py:51
  115.6 12.6 %copy.48 = f32[8,6,64,128]{0,3,2,1:T(8,128)} copy(f32[8,6,64,128]{3,2,0,1:T(8,128)S(1)} %add_bitcast_fusion) | data formatting | bytes 3145728 | tf_op jit(solution)/shard_map/transpose | solution.py:95
  128.2 63.1 %gather_fusion = bf16[16384,8]{1,0:T(8,128)(2,1)} fusion(f32[8,49152]{0,1:T(8,128)} %bitcast.47, s32[16384]{0:T(1024)S(1)} %broadcast_clamp_fusion), kind=kCustom, calls=%fused_computation | custom fusion | bytes 589824 | tf_op jit(solution)/shard_map/gather | solution.py:101
  191.3 6.0 %fusion.8 = f32[128,128,8]{2,1,0:T(8,128)} fusion(bf16[8,128,128]{0,2,1:T(8,128)(2,1)} %bitcast.54, pred[128]{0:T(512)(128)(4,1)S(1)} %iota_compare_fusion.4), kind=kLoop, calls=%fused_computation.29 | loop fusion | flops 262144 | bytes 786560
  197.3 5.4 %copy.74 = f32[128,128,8]{1,2,0:T(8,128)S(1)} copy(f32[128,128,8]{2,1,0:T(8,128)} %fusion.8) | data formatting | bytes 1048576
  203.5 2.5 gather_fusion.1
  206.7 2.7 gather_fusion.2
  210.1 4.8 %copy.73 = f32[128,128,8]{2,1,0:T(8,128)} copy(f32[128,128,8]{1,2,0:T(8,128)S(1)} %multiply_reduce_fusion) | data formatting | bytes 1048576 | tf_op jit(solution)/shard_map/nrck,nrk->nck/dot_general | solution.py:57
  214.9 6.6 %negate_convert_fusion = bf16[128,128,8]{2,1,0:T(8,128)(2,1)} fusion(f32[128,128,8]{2,1,0:T(8,128)} %copy.73), kind=kLoop, calls=%fused_computation.15 | loop fusion | flops 262144 | bytes 786432 | tf_op jit(solution)/shard_map/convert_element_type | solution.py:58
  221.5 95.8 %scatter_custom_fusion = f32[8,49152]{0,1:T(8,128)} fusion(f32[8,49152]{0,1:T(8,128)} %bitcast.48, s32[16384]{0:T(1024)} %bitcast.59, bf16[16384,8]{1,0:T(8,128)(2,1)} %bitcast.53), kind=kCustom, calls=%fused_computation.13 | custom fusion | flops 262144 | bytes 5767168 | tf_op jit(solution)/shard_map/scatter-add | solution.py:126
  317.3 13.4 %copy.49 = f32[8,6,64,128]{3,0,2,1:T(8,128)S(1)} copy(f32[8,6,64,128]{0,3,2,1:T(8,128)} %bitcast.49) | data formatting | bytes 3145728 | tf_op jit(solution)/shard_map/reshape | solution.py:127
  331.1 3.4 collective-permute-start.8
  334.5 1.4 collective-permute-start.9
  336.0 6.0 %fusion.1 = f32[6,8,64,128]{3,2,1,0:T(8,128)} fusion(bf16[6,8,8,64,128]{4,3,2,1,0:T(8,128)(2,1)} %param.14, f32[6,8,64,128]{3,2,1,0:T(8,128)S(1)} %copy.50), kind=kLoop, calls=%fused_computation.10 | loop fusion | flops 9043968 | bytes 9437184 | tf_op jit(solution)/shard_map/reduce_sum | solution.py:51
  342.3 67.9 %psum.7 = f32[8,8]{1,0:T(8,128)S(1)} all-reduce(f32[8,8]{1,0:T(8,128)S(1)} %convolution_bitcast_fusion), channel_id=1, replica_groups=mesh['gx'=8,'gy'=16] {'gx','gy'}, use_global_device_ids=true, to_apply=%region_5.6 | all-reduce | flops 64 | bytes 512 | tf_op jit(solution)/shard_map/psum | solution.py:120
  410.3 1.7 fusion.36
  412.0 2.0 copy.52
  414.7 3.2 collective-permute-start.10
  417.9 2.2 collective-permute-start.11
  420.7 15.3 %copy.58 = f32[8,6,64,128]{3,2,0,1:T(8,128)} copy(f32[8,6,64,128]{0,3,2,1:T(8,128)} %bitcast.50) | data formatting | bytes 3145728 | tf_op jit(solution)/shard_map/reshape | solution.py:127
  436.7 1.9 copy.53
  438.6 3.8 select_maximum_fusion
  442.6 2.9 fusion.10
  445.8 1.9 fusion.3
  447.7 1.7 bitcast_add_fusion
  (102 shorter events, 10.0 us)
Async XLA Ops:
  0.6 29.0 %all-to-all-start.2 = ((bf16[128,8,128]{2,1,0:T(8,128)(2,1)}), bf16[128,8,128]{2,1,0:T(8,128)(2,1)S(1)}, u32[]{:S(2)}, u32[]{:S(2)}) async-start(bf16[128,8,128]{2,1,0:T(8,128)(2,1)} %bitcast.57), calls=%async_computation.2 | async-start | bytes 524288 | tf_op jit(solution)/shard_map/all_to_all | solution.py:113
  12.9 31.3 %collective-permute-start = (f32[6,1,128]{2,1,0:T(1,128)S(1)}, f32[6,1,128]{2,1,0:T(1,128)S(1)}, u32[]{:S(2)}, u32[]{:S(2)}) collective-permute-start(f32[6,1,128]{2,1,0:T(1,128)S(1)} %get-tuple-element.20), channel_id=1, source_target_pairs={{0,1},{1,2},{2,3},{3,4},{4,5},{5,6},{6,7},{7,8},{8,9},{9,10},{10,1... | collective-permute-start | bytes 9224 | tf_op jit(solution)/shard_map/ppermute | solution.py:18
  16.3 27.9 %collective-permute-start.1 = (f32[6,1,128]{2,1,0:T(1,128)S(1)}, f32[6,1,128]{2,1,0:T(1,128)S(1)}, u32[]{:S(2)}, u32[]{:S(2)}) collective-permute-start(f32[6,1,128]{2,1,0:T(1,128)S(1)} %get-tuple-element.21), channel_id=1, source_target_pairs={{1,0},{2,1},{3,2},{4,3},{5,4},{6,5},{7,6},{8,7},{9,8},{10,9},{11,1... | collective-permute-start | bytes 9224 | tf_op jit(solution)/shard_map/ppermute | solution.py:19
  18.4 8.2 %copy-start = (bf16[6,8,8,64,128]{4,3,2,1,0:T(8,128)(2,1)S(1)}, bf16[6,8,8,64,128]{4,3,2,1,0:T(8,128)(2,1)}, u32[]{:S(2)}) copy-start(bf16[6,8,8,64,128]{4,3,2,1,0:T(8,128)(2,1)} %param.14) | copy-start | bytes 18874372
  20.9 5.6 %copy-start.26 = (s32[1,1,16384]{2,1,0:T(1,128)S(1)}, s32[1,1,16384]{2,1,0:T(1,128)}, u32[]{:S(2)}) copy-start(s32[1,1,16384]{2,1,0:T(1,128)} %param.16) | copy-start | bytes 196612
  20.9 50.2 %collective-permute-start.4 = (f32[6,8,1,128]{3,1,2,0:T(8,128)S(1)}, f32[6,8,1,128]{3,1,2,0:T(8,128)S(1)}, u32[]{:S(2)}, u32[]{:S(2)}) collective-permute-start(f32[6,8,1,128]{3,1,2,0:T(8,128)S(1)} %get-tuple-element.8), channel_id=1, source_target_pairs={{0,1},{1,2},{2,3},{3,4},{4,5},{5,6},{6,7},{7,8},{8,9},{9,10},{10,1... | collective-permute-start | bytes 73736 | tf_op jit(solution)/shard_map/ppermute | solution.py:18
  24.9 46.2 %collective-permute-start.5 = (f32[6,8,1,128]{3,1,2,0:T(8,128)S(1)}, f32[6,8,1,128]{3,1,2,0:T(8,128)S(1)}, u32[]{:S(2)}, u32[]{:S(2)}) collective-permute-start(f32[6,8,1,128]{3,1,2,0:T(8,128)S(1)} %get-tuple-element.9), channel_id=1, source_target_pairs={{1,0},{2,1},{3,2},{4,3},{5,4},{6,5},{7,6},{8,7},{9,8},{10,9},{11,1... | collective-permute-start | bytes 73736 | tf_op jit(solution)/shard_map/ppermute | solution.py:19
  26.6 3.0 copy-start.20
  29.6 0.7 copy-start.16
  29.6 13.9 %copy-start.27 = (s32[1,1,128]{2,1,0:T(1,128)S(1)}, s32[1,1,128]{2,1,0:T(1,128)}, u32[]{:S(2)}) copy-start(s32[1,1,128]{2,1,0:T(1,128)} %param.18) | copy-start | bytes 1540
  29.6 14.6 %copy-start.8 = (f32[6,64,128]{2,1,0:T(8,128)S(1)}, f32[6,64,128]{2,1,0:T(8,128)}, u32[]{:S(2)}) copy-start(f32[6,64,128]{2,1,0:T(8,128)} %param.12) | copy-start | bytes 589828
  29.6 20.3 %copy-start.25 = (s32[64,128]{1,0:T(8,128)S(1)}, s32[64,128]{1,0:T(8,128)}, u32[]{:S(2)}) copy-start(s32[64,128]{1,0:T(8,128)} %param.13) | copy-start | bytes 98308
  30.3 64.5 %all-to-all-start = ((bf16[128,8,8,128]{3,2,1,0:T(8,128)(2,1)}), bf16[128,8,8,128]{3,2,1,0:T(8,128)(2,1)}, u32[]{:S(2)}, u32[]{:S(2)}) async-start(bf16[128,8,8,128]{3,2,1,0:T(8,128)(2,1)} %bitcast.55), calls=%async_computation | async-start | bytes 4194304 | tf_op jit(solution)/shard_map/all_to_all | solution.py:111
  44.4 25.6 %collective-permute-start.3 = (f32[6,66,1]{2,1,0:T(8,128)S(1)}, f32[6,66,1]{2,1,0:T(8,128)S(1)}, u32[]{:S(2)}, u32[]{:S(2)}) collective-permute-start(f32[6,66,1]{2,1,0:T(8,128)S(1)} %get-tuple-element.12), channel_id=1, source_target_pairs={{16,0},{32,16},{48,32},{64,48},{80,64},{96,80},{112,96},{17,1},{33... | collective-permute-start | bytes 4760 | tf_op jit(solution)/shard_map/ppermute | solution.py:19
  47.4 22.5 %collective-permute-start.2 = (f32[6,66,1]{2,1,0:T(8,128)S(1)}, f32[6,66,1]{2,1,0:T(8,128)S(1)}, u32[]{:S(2)}, u32[]{:S(2)}) collective-permute-start(f32[6,66,1]{2,1,0:T(8,128)S(1)} %get-tuple-element.13), channel_id=1, source_target_pairs={{0,16},{16,32},{32,48},{48,64},{64,80},{80,96},{96,112},{1,17},{17... | collective-permute-start | bytes 4760 | tf_op jit(solution)/shard_map/ppermute | solution.py:18
  70.0 1.1 copy-start.18
  70.0 1.1 copy-start.19
  71.1 0.6 copy-start.21
  71.7 0.6 copy-start.23
  78.0 9.2 %collective-permute-start.6 = (f32[6,8,66,1]{2,1,3,0:T(8,128)}, f32[6,8,66,1]{2,1,3,0:T(8,128)}, u32[]{:S(2)}, u32[]{:S(2)}) collective-permute-start(f32[6,8,66,1]{2,1,3,0:T(8,128)} %copy.41), channel_id=1, source_target_pairs={{0,16},{16,32},{32,48},{48,64},{64,80},{80,96},{96,112},{1,17},{17... | collective-permute-start | bytes 38024 | tf_op jit(solution)/shard_map/ppermute | solution.py:18
  80.0 5.7 %collective-permute-start.7 = (f32[6,8,66,1]{2,1,3,0:T(8,128)}, f32[6,8,66,1]{2,1,3,0:T(8,128)}, u32[]{:S(2)}, u32[]{:S(2)}) collective-permute-start(f32[6,8,66,1]{2,1,3,0:T(8,128)} %copy.42), channel_id=1, source_target_pairs={{16,0},{32,16},{48,32},{64,48},{80,64},{96,80},{112,96},{17,1},{33... | collective-permute-start | bytes 38024 | tf_op jit(solution)/shard_map/ppermute | solution.py:19
  85.7 4.0 copy-start.22
  85.7 4.0 copy-start.24
  94.8 9.8 %copy-start.9 = (f32[6,64,128]{2,1,0:T(8,128)S(1)}, f32[6,64,128]{2,1,0:T(8,128)}, u32[]{:S(2)}) copy-start(f32[6,64,128]{2,1,0:T(8,128)} %get-tuple-element.14) | copy-start | bytes 589828
  94.8 111.9 %all-to-all-start.1 = ((bf16[128,8,8,128]{3,2,1,0:T(8,128)(2,1)}), bf16[128,8,8,128]{3,2,1,0:T(8,128)(2,1)}, u32[]{:S(2)}, u32[]{:S(2)}) async-start(bf16[128,8,8,128]{3,2,1,0:T(8,128)(2,1)} %bitcast.56), calls=%async_computation.1 | async-start | bytes 4194304 | tf_op jit(solution)/shard_map/all_to_all | solution.py:112
  109.9 5.1 %copy-start.2 = (f32[6,8,64,128]{3,2,1,0:T(8,128)S(1)}, f32[6,8,64,128]{3,2,1,0:T(8,128)}, u32[]{:S(2)}) copy-start(f32[6,8,64,128]{3,2,1,0:T(8,128)} %fusion) | copy-start | bytes 4718596
  109.9 5.1 %copy-start.5 = (f32[6,8,64,128]{3,2,1,0:T(8,128)S(1)}, f32[6,8,64,128]{3,2,1,0:T(8,128)}, u32[]{:S(2)}) copy-start(f32[6,8,64,128]{3,2,1,0:T(8,128)} %param.11) | copy-start | bytes 4718596
  197.3 5.4 %copy-start.17 = (bf16[128,8,128]{2,1,0:T(8,128)(2,1)S(1)}, bf16[128,8,128]{2,1,0:T(8,128)(2,1)}, u32[]{:S(2)}) copy-start(bf16[128,8,128]{2,1,0:T(8,128)(2,1)} %copy-done.16) | copy-start | bytes 786436
  206.7 2.8 copy-start.6
  331.1 79.1 %collective-permute-start.8 = (f32[6,8,1,128]{3,1,2,0:T(8,128)S(1)}, f32[6,8,1,128]{3,1,2,0:T(8,128)S(1)}, u32[]{:S(2)}, u32[]{:S(2)}) collective-permute-start(f32[6,8,1,128]{3,1,2,0:T(8,128)S(1)} %get-tuple-element.6), channel_id=1, source_target_pairs={{0,1},{1,2},{2,3},{3,4},{4,5},{5,6},{6,7},{7,8},{8,9},{9,10},{10,1... | collective-permute-start | bytes 73736 | tf_op jit(solution)/shard_map/ppermute | solution.py:18
  334.5 7.5 %copy-start.7 = (f32[128,128,8]{1,2,0:T(8,128)S(1)}, f32[128,128,8]{1,2,0:T(8,128)}, u32[]{:S(2)}) copy-start(f32[128,128,8]{1,2,0:T(8,128)} %copy-done.6) | copy-start | bytes 1572868
  334.5 75.7 %collective-permute-start.9 = (f32[6,8,1,128]{3,1,2,0:T(8,128)S(1)}, f32[6,8,1,128]{3,1,2,0:T(8,128)S(1)}, u32[]{:S(2)}, u32[]{:S(2)}) collective-permute-start(f32[6,8,1,128]{3,1,2,0:T(8,128)S(1)} %get-tuple-element.7), channel_id=1, source_target_pairs={{1,0},{2,1},{3,2},{4,3},{5,4},{6,5},{7,6},{8,7},{9,8},{10,9},{11,1... | collective-permute-start | bytes 73736 | tf_op jit(solution)/shard_map/ppermute | solution.py:19
  414.7 22.1 %collective-permute-start.10 = (f32[6,8,66,1]{2,1,3,0:T(8,128)S(1)}, f32[6,8,66,1]{2,1,3,0:T(8,128)S(1)}, u32[]{:S(2)}, u32[]{:S(2)}) collective-permute-start(f32[6,8,66,1]{2,1,3,0:T(8,128)S(1)} %copy.51), channel_id=1, source_target_pairs={{0,16},{16,32},{32,48},{48,64},{64,80},{80,96},{96,112},{1,17},{17... | collective-permute-start | bytes 38024 | tf_op jit(solution)/shard_map/ppermute | solution.py:18
  417.9 18.1 %collective-permute-start.11 = (f32[6,8,66,1]{2,1,3,0:T(8,128)S(1)}, f32[6,8,66,1]{2,1,3,0:T(8,128)S(1)}, u32[]{:S(2)}, u32[]{:S(2)}) collective-permute-start(f32[6,8,66,1]{2,1,3,0:T(8,128)S(1)} %copy.52), channel_id=1, source_target_pairs={{16,0},{32,16},{48,32},{64,48},{80,64},{96,80},{112,96},{17,1},{33... | collective-permute-start | bytes 38024 | tf_op jit(solution)/shard_map/ppermute | solution.py:19
  438.6 3.9 copy-start.1
  438.6 3.9 copy-start.10
  438.6 3.9 copy-start.11
  438.6 3.9 copy-start.12
  438.6 3.9 copy-start.13
  438.6 3.9 copy-start.14
  438.6 3.9 copy-start.15
  438.6 7.1 %slice-start = ((s8[6291456]{0:T(1024)(128)(4,1)}), s8[4194304]{0:T(1024)(128)(4,1)S(1)}, s32[]{:S(2)}) async-start(s8[6291456]{0:T(1024)(128)(4,1)} %bitcast.51), calls=%async_computation.3 | async-start | bytes 8388608
  442.5 3.2 slice-start.1
  445.7 1.9 copy-start.3
  445.8 1.9 copy-start.4
where the time goes:
time: 451 us; the launch traced here: 449 us
  other arithmetic  153 us (34%)
  local copies, waits for them, and re-layouts  141 us (31%)
  blocking collectives  67.9 us (15%)
  starting transfers between devices  65.2 us (14%)
  waiting for transfers between devices  20 us (4%)
    scatter-add x1, other arithmetic, shards(): flat_cells = flat_cells.at[:, slot_cells].add(added)  95.8 us
    psum x1, blocking collectives, shards(): interaction_grad = -grad_scale * lax.psum(partial_sum, ('gx', 'gy'))  67.9 us
    gather x1, local copies, waits for them, and re-layouts, shards(): flat_cells[:, slot_cells].reshape(components, block_slots, block_size)  63.1 us
    reshape x2, local copies, waits for them, and re-layouts, shards(): flat_cells.reshape(components, layers, rows_y, cols_x).transpose(1, 0, 2, 3)  28.7 us
    ppermute x6, waiting for transfers between devices, with_halo(): after = lax.ppermute(first, axis, down)  20 us
    ppermute x6, starting transfers between devices, with_halo(): before = lax.ppermute(last, axis, up)  18.5 us
    reduce_sum x4, other arithmetic, blocks_transposed(): return jnp.sum(blocks * source_field[:, :, None], axis=1)  16.1 us
    all_to_all x1, starting transfers between devices, shards(): lax.all_to_all(inverse, ('gx', 'gy'), split_axis=0, concat_axis=0, tiled=...  13.2 us
  transfers between devices with their start and end apart: 15, of which 1 were waited for; matrix products, arithmetic and copies ran while one was open for 34% of the time, Pallas kernels for 0%

commit v1 on v0

v1 whole, which is shorter than its diff:
```python
import functools
import math

import jax
import jax.numpy as jnp
from jax import lax
from jax.experimental import pallas as pl
from jax.experimental.pallas import tpu as pltpu
from jax.sharding import PartitionSpec as P

MESH = pl.DeviceIdType.MESH
F32 = jnp.float32
BF16 = jnp.bfloat16

LAYERS, NC, CY, CX = 6, 8, 64, 128
FIELDS = LAYERS * NC
PAD = 80
WX, WY = 8, 16
DEVICES = WX * WY
BLOCKS, BLK = 128, 128
NB = 8
CHUNKS = BLOCKS // NB
DELAY = 5
ROWS = 16


def kernel(
    cot_h, perm_h, mask_h, diag_h, flux_h, cells_ref, count_ref, helper_ref, inv_h, coup_h, phase_h,
    out_h, grad_ref,
    cot_v, perm_v, mask_v, diag_v, flux_v, inv_v, coup_v, phase_v,
    w_v, k_v, t_v, f16_v, s2_v, code_v, y_v, oh_v, lhs_v,
    ps, rb, cs, cr, g_v, gt, ga, gt2, gb,
    hx_s, hx_r, hy_s, hy_r, out_v,
    load_sem, blk_sem, fl_sem, out_sem,
    halo_send, halo_recv, ps_send, ps_recv, cs_send, cs_recv, g_send, g_recv,
):
    gx = lax.axis_index("gx")
    gy = lax.axis_index("gy")
    me = gx * WY + gy

    def device(linear):
        return (lax.div(linear, WY), lax.rem(linear, WY))

    loads = [
        pltpu.make_async_copy(cot_h, cot_v, load_sem.at[0]),
        pltpu.make_async_copy(perm_h, perm_v, load_sem.at[1]),
        pltpu.make_async_copy(mask_h, mask_v, load_sem.at[2]),
    ]
    for copy in loads:
        copy.start()

    def block_copies(layer):
        return (
            pltpu.make_async_copy(diag_h.at[layer], diag_v.at[layer], blk_sem.at[0, layer]),
            pltpu.make_async_copy(flux_h.at[layer], flux_v.at[layer], blk_sem.at[1, layer]),
        )

    for layer in range(LAYERS):
        for copy in block_copies(layer):
            copy.start()
    flash_loads = [
        pltpu.make_async_copy(inv_h, inv_v, fl_sem.at[0]),
        pltpu.make_async_copy(coup_h, coup_v, fl_sem.at[1]),
        pltpu.make_async_copy(phase_h, phase_v, fl_sem.at[2]),
    ]
    for copy in flash_loads:
        copy.start()

    barrier = pltpu.get_barrier_semaphore()

    def greet(step, carry):
        pl.semaphore_signal(
            barrier, inc=1, device_id=device(lax.rem(me + step, DEVICES)), device_id_type=MESH
        )
        return carry

    lax.fori_loop(1, DEVICES, greet, 0)

    lane_i = lax.broadcasted_iota(jnp.int32, (BLOCKS, BLK), 1)
    row_i = lax.broadcasted_iota(jnp.int32, (BLOCKS, BLK), 0)
    target = lax.rem(row_i + me, DEVICES)
    choose = jnp.where(helper_ref[...] == target, 1.0, 0.0).astype(BF16)
    cells = cells_ref[...]
    cell_layer = lax.shift_right_logical(cells, 13).astype(F32).astype(BF16)
    cell_y = lax.shift_right_logical(cells, 7) & (CY - 1)
    cell_y = jnp.where(row_i < count_ref[0, 0], cell_y, CY).astype(F32).astype(BF16)
    cell_x = (cells & (CX - 1)).astype(F32).astype(BF16)
    code_v[...] = CX * jnp.dot(choose, cell_layer, preferred_element_type=F32) + jnp.dot(
        choose, cell_x, preferred_element_type=F32
    )
    y_v[...] = jnp.dot(choose, cell_y, preferred_element_type=F32)

    w_v[pl.ds(0, NC * PAD), :] = jnp.zeros((NC * PAD, CX), F32)
    w_v[pl.ds((FIELDS + NC) * PAD, NC * PAD), :] = jnp.zeros((NC * PAD, CX), F32)
    k_v[pl.ds(0, PAD), :] = jnp.zeros((PAD, CX), F32)
    k_v[pl.ds((LAYERS + 1) * PAD, PAD), :] = jnp.zeros((PAD, CX), F32)

    for copy in loads:
        copy.wait()

    lane_y = lax.broadcasted_iota(jnp.int32, (CY, CX), 1)
    hole = mask_v[...].astype(F32)
    keep = 1.0 - hole

    def field(q):
        return pl.ds(pl.multiple_of(q * CY, CY), CY)

    def pack_edges(q, value, carry):
        right, left = carry
        turned = pltpu.roll(value, 2 * q + 2, axis=1)
        right = jnp.where(lane_y == 2 * q + 1, turned, right)
        left = jnp.where(lane_y == 2 * q + 2, turned, left)
        return right, left

    def mask_fields(source, which, start):
        def step(q, carry):
            value = source[field(q), :] * keep
            w_v[pl.ds(pl.multiple_of((q + NC) * PAD + 8, 8), CY), :] = value
            return pack_edges(q, value, carry)

        right, left = lax.fori_loop(0, FIELDS, step, start, unroll=2)
        hx_s[which, 0] = left
        hx_s[which, 1] = right
        for layer in range(LAYERS):
            base = (layer + 1) * NC * PAD + 8
            hy_s[which, 0, pl.ds(layer * NC, NC), :] = w_v[pl.ds(base, NC, stride=PAD), :]
            hy_s[which, 1, pl.ds(layer * NC, NC), :] = w_v[pl.ds(base + CY - 1, NC, stride=PAD), :]

    def halo_copies(which):
        east = (lax.rem(gx + 1, WX), gy)
        west = (lax.rem(gx + WX - 1, WX), gy)
        south = (gx, lax.rem(gy + 1, WY))
        north = (gx, lax.rem(gy + WY - 1, WY))
        plan = (
            (hx_s.at[which, 1], hx_r.at[which, 0], east),
            (hx_s.at[which, 0], hx_r.at[which, 1], west),
            (hy_s.at[which, 1], hy_r.at[which, 0], south),
            (hy_s.at[which, 0], hy_r.at[which, 1], north),
        )
        return [
            pltpu.make_async_remote_copy(
                src_ref=source,
                dst_ref=target_ref,
                send_sem=halo_send.at[which, i],
                recv_sem=halo_recv.at[which, i],
                device_id=where,
                device_id_type=MESH,
            )
            for i, (source, target_ref, where) in enumerate(plan)
        ]

    def edge_columns(which):
        odd = lax.rem(lane_y, 2) == 1
        from_west = jnp.where(gx > 0, hx_r[which, 0], 0.0)
        from_east = jnp.where(gx < WX - 1, hx_r[which, 1], 0.0)
        hx_r[which, 0] = jnp.where(odd, from_west, from_east)

    def edge_rows(which):
        for layer in range(LAYERS):
            base = (layer + 1) * NC * PAD
            rows = pl.ds(layer * NC, NC)
            w_v[pl.ds(base + 7, NC, stride=PAD), :] = jnp.where(gy > 0, hy_r[which, 0, rows, :], 0.0)
            w_v[pl.ds(base + 8 + CY, NC, stride=PAD), :] = jnp.where(
                gy < WY - 1, hy_r[which, 1, rows, :], 0.0
            )

    zero_edge = jnp.zeros((CY, CX), F32)
    start = (zero_edge, zero_edge)
    for layer in range(LAYERS):
        value = perm_v[pl.ds(layer * CY, CY), :]
        k_v[pl.ds((layer + 1) * PAD + 8, CY), :] = value
        start = pack_edges(FIELDS + layer, value, start)
    mask_fields(cot_v, 0, start)
    for layer in range(LAYERS):
        base = (layer + 1) * PAD + 8
        hy_s[0, 0, pl.ds(FIELDS + layer, 1), :] = k_v[pl.ds(base, 1), :]
        hy_s[0, 1, pl.ds(FIELDS + layer, 1), :] = k_v[pl.ds(base + CY - 1, 1), :]

    pl.semaphore_wait(barrier, DEVICES - 1)
    first_halo = halo_copies(0)
    for copy in first_halo:
        copy.start()
    for copy in first_halo:
        copy.wait_recv()

    edge_columns(0)
    edge_rows(0)
    for layer in range(LAYERS):
        base = (layer + 1) * PAD
        k_v[pl.ds(base + 7, 1), :] = jnp.where(gy > 0, hy_r[0, 0, pl.ds(FIELDS + layer, 1), :], 0.0)
        k_v[pl.ds(base + 8 + CY, 1), :] = jnp.where(
            gy < WY - 1, hy_r[0, 1, pl.ds(FIELDS + layer, 1), :], 0.0
        )

    def beside_x(value, edges, shift, lane):
        turned = pltpu.roll(edges, shift, axis=1)
        west = pltpu.roll(jnp.where(lane == CX - 1, turned, value), 1, axis=1)
        east = pltpu.roll(jnp.where(lane == 0, turned, value), CX - 1, axis=1)
        return west, east

    def make_weights(layer, carry):
        base = pl.multiple_of((layer + 1) * PAD, 8)
        centre = k_v[pl.ds(base + 8, CY), :]
        west, east = beside_x(centre, hx_r[0, 0], CX - 2 * (FIELDS + layer) - 2, lane_y)
        others = (
            k_v[pl.ds(base + 8 + PAD, CY), :],
            k_v[pl.ds(base + 8 - PAD, CY), :],
            k_v[pl.ds(base + 9, CY), :],
            k_v[pl.ds(base + 7, CY), :],
            east,
            west,
        )
        for i, other in enumerate(others):
            t_v[i, field(layer), :] = 2.0 * centre * other / (centre + other)
        return carry

    lax.fori_loop(0, LAYERS, make_weights, 0)

    lane_r = lax.broadcasted_iota(jnp.int32, (ROWS, CX), 1)

    def blocks(layer, which, source, put):
        for part in range(CY // ROWS):
            r0 = part * ROWS
            rows = pl.ds(pl.multiple_of(layer * CY + r0, ROWS), ROWS)
            weights = [t_v[i, rows, :] for i in range(6)]
            edges = hx_r[which, 0, pl.ds(r0, ROWS), :]
            own, around = [], []
            for c in range(NC):
                base = pl.multiple_of((layer + 1) * (NC * PAD) + (c * PAD + 8 + r0), 8)
                value = w_v[pl.ds(base, ROWS), :]
                shift = CX - 2 * (layer * NC + c) - 2
                west, east = beside_x(value, edges, shift, lane_r)
                total = weights[0] * w_v[pl.ds(base + NC * PAD, ROWS), :]
                total = total + weights[1] * w_v[pl.ds(base - NC * PAD, ROWS), :]
                total = total + weights[2] * w_v[pl.ds(base + 1, ROWS), :]
                total = total + weights[3] * w_v[pl.ds(base - 1, ROWS), :]
                total = total + weights[4] * east
                total = total + weights[5] * west
                own.append(value)
                around.append(total)
            well = mask_v[pl.ds(r0, ROWS), :].astype(F32)
            for c in range(NC):
                frm = pl.ds(pl.multiple_of((layer * NC + c) * CY + r0, ROWS), ROWS)
                acc = well * source[frm, :]
                for r in range(NC):
                    acc = acc + diag_v[layer, r, c, pl.ds(r0, ROWS), :].astype(F32) * own[r]
                    acc = acc - flux_v[layer, r, c, pl.ds(r0, ROWS), :].astype(F32) * around[r]
                put(layer, c, r0, acc)

    def put_first(layer, c, r0, value):
        lanes = pl.ds(pl.multiple_of(layer * CX, CX), CX)
        f16_v[pl.ds(c * CY + r0, ROWS), lanes] = value.astype(BF16)
        s2_v[pl.ds(pl.multiple_of((layer * NC + c) * CY + r0, ROWS), ROWS), :] = value

    def first_layer(layer, carry):
        for copy in block_copies(layer):
            copy.wait()
        blocks(layer, 0, cot_v, put_first)
        return carry

    lax.fori_loop(0, LAYERS, first_layer, 0)
    for copy in flash_loads:
        copy.wait()

    iota_x = lax.broadcasted_iota(jnp.int32, (CX, BLK), 0).astype(F32).astype(BF16)
    iota_y = lax.broadcasted_iota(jnp.int32, (CY, BLK), 0).astype(F32)
    one16 = jnp.ones((CX, BLK), BF16)
    zero16 = jnp.zeros((CX, BLK), BF16)

    def one_hot(p, b):
        code = code_v[pl.ds(p, 1), :]
        for layer in range(LAYERS):
            own_x = jnp.broadcast_to((code - float(layer * CX)).astype(BF16), (CX, BLK))
            oh_v[pl.ds(layer * CX, CX), pl.ds(b * BLK, BLK)] = jnp.where(own_x == iota_x, one16, zero16)

    def send_block(buf, to, p, peer, send, recv, chunk):
        return pltpu.make_async_remote_copy(
            src_ref=buf.at[p],
            dst_ref=to.at[p],
            send_sem=send.at[chunk],
            recv_sem=recv.at[chunk],
            device_id=device(peer),
            device_id_type=MESH,
        )

    def chunk_copy(buf, to, chunk, first, send, recv):
        rows = pl.ds(chunk * NB + first, NB - first)
        return pltpu.make_async_remote_copy(
            src_ref=buf.at[rows],
            dst_ref=to.at[rows],
            send_sem=send.at[chunk],
            recv_sem=recv.at[chunk],
            device_id=device(lax.rem(me + 1, DEVICES)),
            device_id_type=MESH,
        )

    def wait_chunk(buf, to, chunk, send, recv, sent):
        for first in (1, 0):
            @pl.when((chunk == 0) if first else (chunk > 0))
            def _():
                copy = chunk_copy(buf, to, chunk, first, send, recv)
                if sent:
                    copy.wait_send()
                else:
                    copy.wait_recv()

    def gather(chunk):
        for b in range(NB):
            one_hot(chunk * NB + b, b)
        wide = jnp.dot(f16_v[...], oh_v[...], preferred_element_type=F32)
        for b in range(NB):
            p = chunk * NB + b
            hit = jnp.broadcast_to(y_v[pl.ds(p, 1), :], (CY, BLK)) == iota_y
            found = []
            for c in range(NC):
                piece = wide[c * CY : (c + 1) * CY, b * BLK : (b + 1) * BLK]
                found.append(jnp.sum(jnp.where(hit, piece, 0.0), axis=0, keepdims=True))
            picked = jnp.concatenate(found, axis=0).astype(BF16)
            ps[p] = picked
            if b == 0:
                @pl.when(chunk == 0)
                def _():
                    rb[p] = picked

                @pl.when(chunk > 0)
                def _():
                    send_block(ps, rb, p, lax.rem(me + p, DEVICES), ps_send, ps_recv, chunk).start()
            else:
                send_block(ps, rb, p, lax.rem(me + p, DEVICES), ps_send, ps_recv, chunk).start()

    def flash(chunk):
        wait_chunk(ps, rb, chunk, ps_send, ps_recv, False)
        for b in range(NB):
            p = chunk * NB + b
            source = lax.rem(me - p + DEVICES, DEVICES)
            chosen = rb[p].astype(F32)
            multiplier = jnp.sum(inv_v[source].astype(F32) * chosen[:, None, :], axis=0)
            change = -jnp.sum(coup_v[source].astype(F32) * multiplier[:, None, :], axis=0)
            state = phase_v[source].astype(F32)
            g_v[...] += (multiplier * state)[None] * state[:, None, :]
            change = change.astype(BF16)
            cs[p] = change
            if b == 0:
                @pl.when(chunk == 0)
                def _():
                    cr[p] = change

                @pl.when(chunk > 0)
                def _():
                    send_block(cs, cr, p, source, cs_send, cs_recv, chunk).start()
            else:
                send_block(cs, cr, p, source, cs_send, cs_recv, chunk).start()

    def scatter(chunk):
        wait_chunk(cs, cr, chunk, cs_send, cs_recv, False)
        for b in range(NB):
            p = chunk * NB + b
            one_hot(p, b)
            hit = jnp.broadcast_to(y_v[pl.ds(p, 1), :], (CY, BLK)) == iota_y
            change = cr[p].astype(F32)
            for c in range(NC):
                lhs_v[pl.ds(c * CY, CY), pl.ds(b * BLK, BLK)] = jnp.where(
                    hit, jnp.broadcast_to(change[c : c + 1], (CY, BLK)), 0.0
                ).astype(BF16)
        added = lax.dot_general(
            lhs_v[...], oh_v[...], (((1,), (1,)), ((), ())), preferred_element_type=F32
        )
        for layer in range(LAYERS):
            rows = pl.ds(layer * NC * CY, NC * CY)
            s2_v[rows, :] = s2_v[rows, :] + added[:, layer * CX : (layer + 1) * CX]

    g_v[...] = jnp.zeros_like(g_v)

    def loop(low, high, *steps):
        def body(t, carry):
            for step, back in steps:
                step(t - back)
            return carry

        lax.fori_loop(low, high, body, 0)

    loop(0, DELAY, (gather, 0))
    loop(DELAY, CHUNKS, (gather, 0), (flash, DELAY))
    loop(CHUNKS, CHUNKS + DELAY, (flash, DELAY), (scatter, CHUNKS))

    lane_g = lax.broadcasted_iota(jnp.int32, (NC, CX), 1)
    tile = jnp.zeros((NC, CX), F32)
    for j in range(NC):
        tile = jnp.where(lane_g == j, jnp.sum(g_v[j], axis=1, keepdims=True), tile)
    gt[...] = tile
    ga[gx] = tile

    def grad_copy(source, target_ref, where, phase):
        return pltpu.make_async_remote_copy(
            src_ref=source,
            dst_ref=target_ref,
            send_sem=g_send.at[phase],
            recv_sem=g_recv.at[phase],
            device_id=where,
            device_id_type=MESH,
        )

    def send_x(step, carry):
        grad_copy(gt, ga.at[gx], (lax.rem(gx + step, WX), gy), 0).start()
        return carry

    lax.fori_loop(1, WX, send_x, 0)

    loop(CHUNKS + DELAY, 2 * CHUNKS, (scatter, CHUNKS))

    some = ga.at[pl.ds(0, WX - 1)]
    grad_copy(some, some, (lax.rem(gx + 1, WX), gy), 0).wait_recv()
    part = ga[0]
    for i in range(1, WX):
        part = part + ga[i]
    gt2[...] = part
    gb[gy] = part

    def send_y(step, carry):
        grad_copy(gt2, gb.at[gy], (gx, lax.rem(gy + step, WY)), 1).start()
        return carry

    lax.fori_loop(1, WY, send_y, 0)

    mask_fields(s2_v, 1, (zero_edge, zero_edge))
    second_halo = halo_copies(1)
    for copy in second_halo:
        copy.start()
    for copy in second_halo:
        copy.wait_recv()
    edge_columns(1)
    edge_rows(1)

    def put_second(layer, c, r0, value):
        out_v[pl.ds(pl.multiple_of((layer * NC + c) * CY + r0, ROWS), ROWS), :] = value

    def out_copy(layer):
        rows = pl.ds(pl.multiple_of(layer * NC * CY, NC * CY), NC * CY)
        return pltpu.make_async_copy(out_v.at[rows], out_h.at[rows], out_sem.at[layer])

    def second_layer(layer, carry):
        blocks(layer, 1, s2_v, put_second)
        out_copy(layer).start()
        return carry

    lax.fori_loop(0, LAYERS, second_layer, 0)

    some = gb.at[pl.ds(0, WY - 1)]
    grad_copy(some, some, (gx, lax.rem(gy + 1, WY)), 1).wait_recv()
    total = gb[0]
    for i in range(1, WY):
        total = total + gb[i]
    scale = -1.0 / math.sqrt(BLK * BLOCKS * DEVICES)
    grad_ref[...] = scale * total[:, :NC]

    for copy in first_halo + second_halo:
        copy.wait_send()
    some = ga.at[pl.ds(0, WX - 1)]
    grad_copy(some, some, (lax.rem(gx + 1, WX), gy), 0).wait_send()
    some = gb.at[pl.ds(0, WY - 1)]
    grad_copy(some, some, (gx, lax.rem(gy + 1, WY)), 1).wait_send()

    def drain(chunk, carry):
        wait_chunk(ps, rb, chunk, ps_send, ps_recv, True)
        wait_chunk(cs, cr, chunk, cs_send, cs_recv, True)
        return carry

    lax.fori_loop(0, CHUNKS, drain, 0)

    def drain_out(layer, carry):
        out_copy(layer).wait()
        return carry

    lax.fori_loop(0, LAYERS, drain_out, 0)


def shards(
    cotangent, permeability, well_mask, diag_block, flux_block, cell_list, block_count, helper_of,
    flash_inverse, flash_coupling, phase_state,
):
    any_space = pl.BlockSpec(memory_space=pl.ANY)
    vmem = pl.BlockSpec(memory_space=pltpu.VMEM)
    smem = pl.BlockSpec(memory_space=pltpu.SMEM)
    dma = pltpu.SemaphoreType.DMA
    adjoint, grad = pl.pallas_call(
        kernel,
        out_shape=(
            jax.ShapeDtypeStruct((FIELDS * CY, CX), F32),
            jax.ShapeDtypeStruct((NC, NC), F32),
        ),
        in_specs=[any_space] * 5 + [vmem, smem, vmem] + [any_space] * 3,
        out_specs=(any_space, vmem),
        scratch_shapes=[
            pltpu.VMEM((FIELDS * CY, CX), F32),
            pltpu.VMEM((LAYERS * CY, CX), F32),
            pltpu.VMEM((CY, CX), jnp.int32),
            pltpu.VMEM((LAYERS, NC, NC, CY, CX), BF16),
            pltpu.VMEM((LAYERS, NC, NC, CY, CX), BF16),
            pltpu.VMEM((BLOCKS, NC, NC, BLK), BF16),
            pltpu.VMEM((BLOCKS, NC, NC, BLK), BF16),
            pltpu.VMEM((BLOCKS, NC, BLK), BF16),
            pltpu.VMEM(((FIELDS + 2 * NC) * PAD, CX), F32),
            pltpu.VMEM(((LAYERS + 2) * PAD, CX), F32),
            pltpu.VMEM((6, LAYERS * CY, CX), F32),
            pltpu.VMEM((NC * CY, LAYERS * CX), BF16),
            pltpu.VMEM((FIELDS * CY, CX), F32),
            pltpu.VMEM((BLOCKS, BLK), F32),
            pltpu.VMEM((BLOCKS, BLK), F32),
            pltpu.VMEM((LAYERS * CX, NB * BLK), BF16),
            pltpu.VMEM((NC * CY, NB * BLK), BF16),
            pltpu.VMEM((BLOCKS, NC, BLK), BF16),
            pltpu.VMEM((BLOCKS, NC, BLK), BF16),
            pltpu.VMEM((BLOCKS, NC, BLK), BF16),
            pltpu.VMEM((BLOCKS, NC, BLK), BF16),
            pltpu.VMEM((NC, NC, BLK), F32),
            pltpu.VMEM((NC, CX), F32),
            pltpu.VMEM((WX, NC, CX), F32),
            pltpu.VMEM((NC, CX), F32),
            pltpu.VMEM((WY, NC, CX), F32),
            pltpu.VMEM((2, 2, CY, CX), F32),
            pltpu.VMEM((2, 2, CY, CX), F32),
            pltpu.VMEM((2, 2, 56, CX), F32),
            pltpu.VMEM((2, 2, 56, CX), F32),
            pltpu.VMEM((FIELDS * CY, CX), F32),
            dma((3,)),
            dma((2, LAYERS)),
            dma((3,)),
            dma((LAYERS,)),
            dma((2, 4)),
            dma((2, 4)),
            dma((CHUNKS,)),
            dma((CHUNKS,)),
            dma((CHUNKS,)),
            dma((CHUNKS,)),
            dma((2,)),
            dma((2,)),
        ],
        compiler_params=pltpu.CompilerParams(
            collective_id=0, has_side_effects=True, vmem_limit_bytes=60 << 20
        ),
    )(
        cotangent.reshape(FIELDS * CY, CX),
        permeability.reshape(LAYERS * CY, CX),
        well_mask,
        diag_block,
        flux_block,
        cell_list.reshape(BLOCKS, BLK),
        block_count,
        helper_of.reshape(1, BLOCKS),
        flash_inverse.reshape(BLOCKS, NC, NC, BLK),
        flash_coupling.reshape(BLOCKS, NC, NC, BLK),
        phase_state.reshape(BLOCKS, NC, BLK),
    )
    return adjoint.reshape(cotangent.shape), grad


def solution(mesh):
    return jax.shard_map(
        shards,
        mesh=mesh,
        in_specs=(
            P(None, None, "gy", "gx"),
            P(None, "gy", "gx"),
            P("gy", "gx"),
            P(None, None, None, "gy", "gx"),
            P(None, None, None, "gy", "gx"),
            P("gy", "gx", None),
            P("gy", "gx"),
            P("gy", "gx", None),
            P("gy", "gx", None, None, None, None),
            P("gy", "gx", None, None, None, None),
            P("gy", "gx", None, None, None),
        ),
        out_specs=(P(None, None, "gy", "gx"), P()),
        check_vma=False,
    )
```

time: 451 us -> 90.9 us (0.20)
  other arithmetic: 153 us -> 0 us
  local copies, waits for them, and re-layouts: 141 us -> 3.32 us
  Pallas kernels: 0 us -> 86.1 us
  blocking collectives: 67.9 us -> 0 us
  starting transfers between devices: 65.2 us -> 0 us
  waiting for transfers between devices: 20 us -> 0 us
    scatter-add x1 -> x0, other arithmetic: 95.8 us -> none  [shards(): flat_cells = flat_cells.at[:, slot_cells].add(added)]
    pallas_call x0 -> x1, Pallas kernels: none -> 86.1 us  [shards(): pl.pallas_call(kernel, out_shape=(jax.ShapeDtypeStruct((FIELDS * CY, CX),...]
    gather x4 -> x0, local copies, waits for them, and re-layouts: 69.1 us -> none  [the longest x1 63.1 us: shards(): flat_cells[:, slot_cells].reshape(components, block_slots, block_size)]
    psum x1 -> x0, blocking collectives: 67.9 us -> none  [shards(): interaction_grad = -grad_scale * lax.psum(partial_sum, ('gx', 'gy'))]
    all_to_all x3 -> x0, starting transfers between devices: 34.5 us -> none  [the longest x1 13.2 us: shards(): lax.all_to_all(inverse, ('gx', 'gy'), split_axis=0, concat_axis=0, tiled=...]
    ppermute x12 -> x0, starting transfers between devices: 30.7 us -> none  [the longest x6 18.5 us: with_halo(): before = lax.ppermute(last, axis, up)]
    reshape x2 -> x0, local copies, waits for them, and re-layouts: 28.7 us -> none  [shards(): flat_cells.reshape(components, layers, rows_y, cols_x).transpose(1, 0, 2, 3)]
    ppermute x12 -> x0, waiting for transfers between devices: 20 us -> none  [the longest x6 20 us: with_halo(): after = lax.ppermute(first, axis, down)]
  transfers between devices with their start and end apart: 15 -> 0, of which waited for: 1 -> 0; matrix products, arithmetic and copies ran while one was open for 34% -> 0% of each run, Pallas kernels for 0% -> 0%
where the time goes in v1:
time: 90.9 us; the launch traced here: 90.7 us
  Pallas kernels  86.1 us (95%)
  local copies, waits for them, and re-layouts  3.32 us (4%)
  between operations  1.3 us (1%)
    pallas_call x1, Pallas kernels, shards(): pl.pallas_call(kernel, out_shape=(jax.ShapeDtypeStruct((FIELDS * CY, CX),...  86.1 us
    unnamed x4, local copies, waits for them, and re-layouts  3.32 us

profile of v1, /device:TPU:1, one launch (start us, length us, event | category | flops | bytes accessed | tf_op | source)
XLA Modules:
  0.0 90.7 jit_solution(2429085602385350871)
XLA Ops:
  1.3 86.1 %shard_map.122 = (f32[3072,128]{1,0:T(8,128)}, f32[8,8]{1,0:T(8,128)}) custom-call(f32[3072,128]{1,0:T(8,128)} %bitcast.10, f32[384,128]{1,0:T(8,128)} %bitcast.13, s32[64,128]{1,0:T(8,128)} %mask_h.1, bf16[6,8,8,64,128]{4,3,2,1,0:T(8,128)(2,1)} %diag_h.1, bf16[6,8,8,64,128]{4,3,2,1,0:T(8,128)(2,1)} %flux_h.1, s32[128,128]{1,0:T(8,128)} %bitcast.14, ...), custom_call_target="tpu_custom_call" | custom-call | tf_op jit(solution)/shard_map/pallas_call | solution.py:485
  87.3 0.0 copy-start
  87.4 2.7 %copy.16 = f32[6,8,64,128]{3,2,1,0:T(8,128)} copy(f32[6,8,64,128]{3,2,1,0:T(8,128)} %bitcast.11) | data formatting | bytes 3145728
  90.1 0.0 copy-done
  90.1 0.6 copy.17
Async XLA Ops:
  87.3 2.7 %copy-start = (f32[8,8]{1,0:T(8,128)S(1)}, f32[8,8]{1,0:T(8,128)}, u32[]{:S(2)}) copy-start(f32[8,8]{1,0:T(8,128)} %get-tuple-element.9) | copy-start | bytes 772

commit v2 on v1

--- a/solution.py
+++ b/solution.py
@@ -25,13 +25,13 @@
 
 
 def kernel(
-    cot_h, perm_h, mask_h, diag_h, flux_h, cells_ref, count_ref, helper_ref, inv_h, coup_h, phase_h,
-    out_h, grad_ref,
-    cot_v, perm_v, mask_v, diag_v, flux_v, inv_v, coup_v, phase_v,
+    cot_h, perm_h, mask_h, diag_h, flux_h, cells_h, count_ref, helper_h, inv_h, coup_h, phase_h,
+    out_v, grad_ref,
+    cot_v, perm_v, mask_v, cells_ref, helper_ref, diag_v, flux_v, inv_v, coup_v, phase_v,
     w_v, k_v, t_v, f16_v, s2_v, code_v, y_v, oh_v, lhs_v,
     ps, rb, cs, cr, g_v, gt, ga, gt2, gb,
-    hx_s, hx_r, hy_s, hy_r, out_v,
-    load_sem, blk_sem, fl_sem, out_sem,
+    hx_s, hx_r, hy_s, hy_r,
+    load_sem, blk_sem, fl_sem,
     halo_send, halo_recv, ps_send, ps_recv, cs_send, cs_recv, g_send, g_recv,
 ):
     gx = lax.axis_index("gx")
@@ -46,18 +46,20 @@
         pltpu.make_async_copy(perm_h, perm_v, load_sem.at[1]),
         pltpu.make_async_copy(mask_h, mask_v, load_sem.at[2]),
     ]
-    for copy in loads:
+    table_loads = [
+        pltpu.make_async_copy(cells_h, cells_ref, load_sem.at[3]),
+        pltpu.make_async_copy(helper_h, helper_ref, load_sem.at[4]),
+    ]
+    for copy in loads + table_loads:
         copy.start()
 
-    def block_copies(layer):
-        return (
-            pltpu.make_async_copy(diag_h.at[layer], diag_v.at[layer], blk_sem.at[0, layer]),
-            pltpu.make_async_copy(flux_h.at[layer], flux_v.at[layer], blk_sem.at[1, layer]),
-        )
-
-    for layer in range(LAYERS):
-        for copy in block_copies(layer):
-            copy.start()
+    def block_copy(which, layer):
+        source, held = ((diag_h, diag_v), (flux_h, flux_v))[which]
+        return pltpu.make_async_copy(source.at[layer], held.at[layer], blk_sem.at[which, layer])
+
+    for which in range(2):
+        for layer in range(LAYERS):
+            block_copy(which, layer).start()
     flash_loads = [
         pltpu.make_async_copy(inv_h, inv_v, fl_sem.at[0]),
         pltpu.make_async_copy(coup_h, coup_v, fl_sem.at[1]),
@@ -76,9 +78,11 @@
 
     lax.fori_loop(1, DEVICES, greet, 0)
 
+    for copy in table_loads:
+        copy.wait()
     lane_i = lax.broadcasted_iota(jnp.int32, (BLOCKS, BLK), 1)
     row_i = lax.broadcasted_iota(jnp.int32, (BLOCKS, BLK), 0)
-    target = lax.rem(row_i + me, DEVICES)
+    target = lax.rem(row_i + me + 1, DEVICES)
     choose = jnp.where(helper_ref[...] == target, 1.0, 0.0).astype(BF16)
     cells = cells_ref[...]
     cell_layer = lax.shift_right_logical(cells, 13).astype(F32).astype(BF16)
@@ -180,17 +184,6 @@
     first_halo = halo_copies(0)
     for copy in first_halo:
         copy.start()
-    for copy in first_halo:
-        copy.wait_recv()
-
-    edge_columns(0)
-    edge_rows(0)
-    for layer in range(LAYERS):
-        base = (layer + 1) * PAD
-        k_v[pl.ds(base + 7, 1), :] = jnp.where(gy > 0, hy_r[0, 0, pl.ds(FIELDS + layer, 1), :], 0.0)
-        k_v[pl.ds(base + 8 + CY, 1), :] = jnp.where(
-            gy < WY - 1, hy_r[0, 1, pl.ds(FIELDS + layer, 1), :], 0.0
-        )
 
     def beside_x(value, edges, shift, lane):
         turned = pltpu.roll(edges, shift, axis=1)
@@ -214,51 +207,73 @@
             t_v[i, field(layer), :] = 2.0 * centre * other / (centre + other)
         return carry
 
-    lax.fori_loop(0, LAYERS, make_weights, 0)
-
     lane_r = lax.broadcasted_iota(jnp.int32, (ROWS, CX), 1)
 
-    def blocks(layer, which, source, put):
-        for part in range(CY // ROWS):
-            r0 = part * ROWS
+    def part_rows(layer, c, r0):
+        return pl.ds(pl.multiple_of((layer * NC + c) * CY + r0, ROWS), ROWS)
+
+    def diag_pass(layer, source, held):
+        for r0 in range(0, CY, ROWS):
+            well = mask_v[pl.ds(r0, ROWS), :].astype(F32)
+            acc = [well * source[part_rows(layer, c, r0), :] for c in range(NC)]
+            for r in range(NC):
+                base = pl.multiple_of((layer + 1) * (NC * PAD) + (r * PAD + 8 + r0), 8)
+                own = w_v[pl.ds(base, ROWS), :]
+                for c in range(NC):
+                    acc[c] = acc[c] + diag_v[layer, r, c, pl.ds(r0, ROWS), :].astype(F32) * own
+            for c in range(NC):
+                held[part_rows(layer, c, r0), :] = acc[c]
+
+    def flux_pass(layer, which, held, put):
+        for r0 in range(0, CY, ROWS):
             rows = pl.ds(pl.multiple_of(layer * CY + r0, ROWS), ROWS)
             weights = [t_v[i, rows, :] for i in range(6)]
             edges = hx_r[which, 0, pl.ds(r0, ROWS), :]
-            own, around = [], []
-            for c in range(NC):
-                base = pl.multiple_of((layer + 1) * (NC * PAD) + (c * PAD + 8 + r0), 8)
+            acc = [held[part_rows(layer, c, r0), :] for c in range(NC)]
+            for r in range(NC):
+                base = pl.multiple_of((layer + 1) * (NC * PAD) + (r * PAD + 8 + r0), 8)
                 value = w_v[pl.ds(base, ROWS), :]
-                shift = CX - 2 * (layer * NC + c) - 2
-                west, east = beside_x(value, edges, shift, lane_r)
+                west, east = beside_x(value, edges, CX - 2 * (layer * NC + r) - 2, lane_r)
                 total = weights[0] * w_v[pl.ds(base + NC * PAD, ROWS), :]
                 total = total + weights[1] * w_v[pl.ds(base - NC * PAD, ROWS), :]
                 total = total + weights[2] * w_v[pl.ds(base + 1, ROWS), :]
                 total = total + weights[3] * w_v[pl.ds(base - 1, ROWS), :]
                 total = total + weights[4] * east
                 total = total + weights[5] * west
-                own.append(value)
-                around.append(total)
-            well = mask_v[pl.ds(r0, ROWS), :].astype(F32)
+                for c in range(NC):
+                    acc[c] = acc[c] - flux_v[layer, r, c, pl.ds(r0, ROWS), :].astype(F32) * total
             for c in range(NC):
-                frm = pl.ds(pl.multiple_of((layer * NC + c) * CY + r0, ROWS), ROWS)
-                acc = well * source[frm, :]
-                for r in range(NC):
-                    acc = acc + diag_v[layer, r, c, pl.ds(r0, ROWS), :].astype(F32) * own[r]
-                    acc = acc - flux_v[layer, r, c, pl.ds(r0, ROWS), :].astype(F32) * around[r]
-                put(layer, c, r0, acc)
+                put(layer, c, r0, acc[c])
 
     def put_first(layer, c, r0, value):
         lanes = pl.ds(pl.multiple_of(layer * CX, CX), CX)
         f16_v[pl.ds(c * CY + r0, ROWS), lanes] = value.astype(BF16)
-        s2_v[pl.ds(pl.multiple_of((layer * NC + c) * CY + r0, ROWS), ROWS), :] = value
-
-    def first_layer(layer, carry):
-        for copy in block_copies(layer):
-            copy.wait()
-        blocks(layer, 0, cot_v, put_first)
-        return carry
-
-    lax.fori_loop(0, LAYERS, first_layer, 0)
+        s2_v[part_rows(layer, c, r0), :] = value
+
+    def first_diag(layer, carry):
+        block_copy(0, layer).wait()
+        diag_pass(layer, cot_v, s2_v)
+        return carry
+
+    def first_flux(layer, carry):
+        block_copy(1, layer).wait()
+        flux_pass(layer, 0, s2_v, put_first)
+        return carry
+
+    lax.fori_loop(0, LAYERS, first_diag, 0)
+
+    for copy in first_halo:
+        copy.wait_recv()
+    edge_columns(0)
+    edge_rows(0)
+    for layer in range(LAYERS):
+        base = (layer + 1) * PAD
+        k_v[pl.ds(base + 7, 1), :] = jnp.where(gy > 0, hy_r[0, 0, pl.ds(FIELDS + layer, 1), :], 0.0)
+        k_v[pl.ds(base + 8 + CY, 1), :] = jnp.where(
+            gy < WY - 1, hy_r[0, 1, pl.ds(FIELDS + layer, 1), :], 0.0
+        )
+    lax.fori_loop(0, LAYERS, make_weights, 0)
+    lax.fori_loop(0, LAYERS, first_flux, 0)
     for copy in flash_loads:
         copy.wait()
 
@@ -273,18 +288,31 @@
             own_x = jnp.broadcast_to((code - float(layer * CX)).astype(BF16), (CX, BLK))
             oh_v[pl.ds(layer * CX, CX), pl.ds(b * BLK, BLK)] = jnp.where(own_x == iota_x, one16, zero16)
 
-    def send_block(buf, to, p, peer, send, recv, chunk):
-        return pltpu.make_async_remote_copy(
-            src_ref=buf.at[p],
-            dst_ref=to.at[p],
-            send_sem=send.at[chunk],
-            recv_sem=recv.at[chunk],
-            device_id=device(peer),
-            device_id_type=MESH,
-        )
-
-    def chunk_copy(buf, to, chunk, first, send, recv):
-        rows = pl.ds(chunk * NB + first, NB - first)
+    def send_chunk(buf, to, chunk, sign, send, recv):
+        for b in range(NB):
+            p = chunk * NB + b
+
+            def remote():
+                pltpu.make_async_remote_copy(
+                    src_ref=buf.at[p],
+                    dst_ref=to.at[p],
+                    send_sem=send.at[chunk],
+                    recv_sem=recv.at[chunk],
+                    device_id=device(lax.rem(me + sign * (p + 1) + DEVICES, DEVICES)),
+                    device_id_type=MESH,
+                ).start()
+
+            if b < NB - 1:
+                remote()
+            else:
+                pl.when(chunk < CHUNKS - 1)(remote)
+
+                @pl.when(chunk == CHUNKS - 1)
+                def _():
+                    pltpu.make_async_copy(buf.at[p], to.at[p], recv.at[chunk]).start()
+
+    def chunk_copy(buf, to, chunk, count, send, recv):
+        rows = pl.ds(chunk * NB, count)
         return pltpu.make_async_remote_copy(
             src_ref=buf.at[rows],
             dst_ref=to.at[rows],
@@ -293,16 +321,6 @@
             device_id=device(lax.rem(me + 1, DEVICES)),
             device_id_type=MESH,
         )
-
-    def wait_chunk(buf, to, chunk, send, recv, sent):
-        for first in (1, 0):
-            @pl.when((chunk == 0) if first else (chunk > 0))
-            def _():
-                copy = chunk_copy(buf, to, chunk, first, send, recv)
-                if sent:
-                    copy.wait_send()
-                else:
-                    copy.wait_recv()
 
     def gather(chunk):
         for b in range(NB):
@@ -315,44 +333,22 @@
             for c in range(NC):
                 piece = wide[c * CY : (c + 1) * CY, b * BLK : (b + 1) * BLK]
                 found.append(jnp.sum(jnp.where(hit, piece, 0.0), axis=0, keepdims=True))
-            picked = jnp.concatenate(found, axis=0).astype(BF16)
-            ps[p] = picked
-            if b == 0:
-                @pl.when(chunk == 0)
-                def _():
-                    rb[p] = picked
-
-                @pl.when(chunk > 0)
-                def _():
-                    send_block(ps, rb, p, lax.rem(me + p, DEVICES), ps_send, ps_recv, chunk).start()
-            else:
-                send_block(ps, rb, p, lax.rem(me + p, DEVICES), ps_send, ps_recv, chunk).start()
+            ps[p] = jnp.concatenate(found, axis=0).astype(BF16)
 
     def flash(chunk):
-        wait_chunk(ps, rb, chunk, ps_send, ps_recv, False)
+        total = g_v[...]
         for b in range(NB):
             p = chunk * NB + b
-            source = lax.rem(me - p + DEVICES, DEVICES)
+            source = lax.rem(me - (p + 1) + DEVICES, DEVICES)
             chosen = rb[p].astype(F32)
             multiplier = jnp.sum(inv_v[source].astype(F32) * chosen[:, None, :], axis=0)
             change = -jnp.sum(coup_v[source].astype(F32) * multiplier[:, None, :], axis=0)
             state = phase_v[source].astype(F32)
-            g_v[...] += (multiplier * state)[None] * state[:, None, :]
-            change = change.astype(BF16)
-            cs[p] = change
-            if b == 0:
-                @pl.when(chunk == 0)
-                def _():
-                    cr[p] = change
-
-                @pl.when(chunk > 0)
-                def _():
-                    send_block(cs, cr, p, source, cs_send, cs_recv, chunk).start()
-            else:
-                send_block(cs, cr, p, source, cs_send, cs_recv, chunk).start()
+            total = total + (multiplier * state)[None] * state[:, None, :]
+            cs[p] = change.astype(BF16)
+        g_v[...] = total
 
     def scatter(chunk):
-        wait_chunk(cs, cr, chunk, cs_send, cs_recv, False)
         for b in range(NB):
             p = chunk * NB + b
             one_hot(p, b)
@@ -371,17 +367,29 @@
 
     g_v[...] = jnp.zeros_like(g_v)
 
-    def loop(low, high, *steps):
+    def loop(low, high, gathers=None, flashes=None, scatters=None):
         def body(t, carry):
-            for step, back in steps:
-                step(t - back)
+            if flashes is not None:
+                chunk_copy(ps, rb, t - flashes, NB, ps_send, ps_recv).wait_recv()
+            if scatters is not None:
+                chunk_copy(cs, cr, t - scatters, NB, cs_send, cs_recv).wait_recv()
+            if gathers is not None:
+                gather(t - gathers)
+            if flashes is not None:
+                flash(t - flashes)
+            if scatters is not None:
+                scatter(t - scatters)
+            if gathers is not None:
+                send_chunk(ps, rb, t - gathers, 1, ps_send, ps_recv)
+            if flashes is not None:
+                send_chunk(cs, cr, t - flashes, -1, cs_send, cs_recv)
             return carry
 
         lax.fori_loop(low, high, body, 0)
 
-    loop(0, DELAY, (gather, 0))
-    loop(DELAY, CHUNKS, (gather, 0), (flash, DELAY))
-    loop(CHUNKS, CHUNKS + DELAY, (flash, DELAY), (scatter, CHUNKS))
+    loop(0, DELAY, gathers=0)
+    loop(DELAY, CHUNKS, gathers=0, flashes=DELAY)
+    loop(CHUNKS, CHUNKS + DELAY, flashes=DELAY, scatters=CHUNKS)
 
     lane_g = lax.broadcasted_iota(jnp.int32, (NC, CX), 1)
     tile = jnp.zeros((NC, CX), F32)
@@ -406,7 +414,7 @@
 
     lax.fori_loop(1, WX, send_x, 0)
 
-    loop(CHUNKS + DELAY, 2 * CHUNKS, (scatter, CHUNKS))
+    loop(CHUNKS + DELAY, 2 * CHUNKS, scatters=CHUNKS)
 
     some = ga.at[pl.ds(0, WX - 1)]
     grad_copy(some, some, (lax.rem(gx + 1, WX), gy), 0).wait_recv()
@@ -426,24 +434,25 @@
     second_halo = halo_copies(1)
     for copy in second_halo:
         copy.start()
+
+    def second_diag(layer, carry):
+        diag_pass(layer, s2_v, out_v)
+        return carry
+
+    lax.fori_loop(0, LAYERS, second_diag, 0)
     for copy in second_halo:
         copy.wait_recv()
     edge_columns(1)
     edge_rows(1)
 
     def put_second(layer, c, r0, value):
-        out_v[pl.ds(pl.multiple_of((layer * NC + c) * CY + r0, ROWS), ROWS), :] = value
-
-    def out_copy(layer):
-        rows = pl.ds(pl.multiple_of(layer * NC * CY, NC * CY), NC * CY)
-        return pltpu.make_async_copy(out_v.at[rows], out_h.at[rows], out_sem.at[layer])
-
-    def second_layer(layer, carry):
-        blocks(layer, 1, s2_v, put_second)
-        out_copy(layer).start()
-        return carry
-
-    lax.fori_loop(0, LAYERS, second_layer, 0)
+        out_v[part_rows(layer, c, r0), :] = value
+
+    def second_flux(layer, carry):
+        flux_pass(layer, 1, out_v, put_second)
+        return carry
+
+    lax.fori_loop(0, LAYERS, second_flux, 0)
 
     some = gb.at[pl.ds(0, WY - 1)]
     grad_copy(some, some, (gx, lax.rem(gy + 1, WY)), 1).wait_recv()
@@ -461,39 +470,40 @@
     grad_copy(some, some, (gx, lax.rem(gy + 1, WY)), 1).wait_send()
 
     def drain(chunk, carry):
-        wait_chunk(ps, rb, chunk, ps_send, ps_recv, True)
-        wait_chunk(cs, cr, chunk, cs_send, cs_recv, True)
-        return carry
-
-    lax.fori_loop(0, CHUNKS, drain, 0)
-
-    def drain_out(layer, carry):
-        out_copy(layer).wait()
-        return carry
-
-    lax.fori_loop(0, LAYERS, drain_out, 0)
+        chunk_copy(ps, rb, chunk, NB, ps_send, ps_recv).wait_send()
+        chunk_copy(cs, cr, chunk, NB, cs_send, cs_recv).wait_send()
+        return carry
+
+    lax.fori_loop(0, CHUNKS - 1, drain, 0)
+    chunk_copy(ps, rb, CHUNKS - 1, NB - 1, ps_send, ps_recv).wait_send()
+    chunk_copy(cs, cr, CHUNKS - 1, NB - 1, cs_send, cs_recv).wait_send()
 
 
 def shards(
     cotangent, permeability, well_mask, diag_block, flux_block, cell_list, block_count, helper_of,
     flash_inverse, flash_coupling, phase_state,
 ):
-    any_space = pl.BlockSpec(memory_space=pl.ANY)
+    hbm = pl.BlockSpec(memory_space=pltpu.HBM)
+    smem = pl.BlockSpec(memory_space=pltpu.SMEM)
     vmem = pl.BlockSpec(memory_space=pltpu.VMEM)
-    smem = pl.BlockSpec(memory_space=pltpu.SMEM)
     dma = pltpu.SemaphoreType.DMA
+    def pin(array):
+        return pltpu.with_memory_space_constraint(array, pltpu.HBM)
+
     adjoint, grad = pl.pallas_call(
         kernel,
         out_shape=(
-            jax.ShapeDtypeStruct((FIELDS * CY, CX), F32),
-            jax.ShapeDtypeStruct((NC, NC), F32),
+            pltpu.VMEM((FIELDS * CY, CX), F32),
+            pltpu.VMEM((NC, NC), F32),
         ),
-        in_specs=[any_space] * 5 + [vmem, smem, vmem] + [any_space] * 3,
-        out_specs=(any_space, vmem),
+        in_specs=[hbm] * 6 + [smem] + [hbm] * 4,
+        out_specs=(vmem, vmem),
         scratch_shapes=[
             pltpu.VMEM((FIELDS * CY, CX), F32),
             pltpu.VMEM((LAYERS * CY, CX), F32),
             pltpu.VMEM((CY, CX), jnp.int32),
+            pltpu.VMEM((BLOCKS, BLK), jnp.int32),
+            pltpu.VMEM((1, BLOCKS), jnp.int32),
             pltpu.VMEM((LAYERS, NC, NC, CY, CX), BF16),
             pltpu.VMEM((LAYERS, NC, NC, CY, CX), BF16),
             pltpu.VMEM((BLOCKS, NC, NC, BLK), BF16),
@@ -521,11 +531,9 @@
             pltpu.VMEM((2, 2, CY, CX), F32),
             pltpu.VMEM((2, 2, 56, CX), F32),
             pltpu.VMEM((2, 2, 56, CX), F32),
-            pltpu.VMEM((FIELDS * CY, CX), F32),
-            dma((3,)),
+            dma((5,)),
             dma((2, LAYERS)),
             dma((3,)),
-            dma((LAYERS,)),
             dma((2, 4)),
             dma((2, 4)),
             dma((CHUNKS,)),
@@ -536,20 +544,20 @@
             dma((2,)),
         ],
         compiler_params=pltpu.CompilerParams(
-            collective_id=0, has_side_effects=True, vmem_limit_bytes=60 << 20
+            collective_id=0, has_side_effects=True, vmem_limit_bytes=50 << 20
         ),
     )(
-        cotangent.reshape(FIELDS * CY, CX),
-        permeability.reshape(LAYERS * CY, CX),
-        well_mask,
-        diag_block,
-        flux_block,
-        cell_list.reshape(BLOCKS, BLK),
+        pin(cotangent.reshape(FIELDS * CY, CX)),
+        pin(permeability.reshape(LAYERS * CY, CX)),
+        pin(well_mask),
+        pin(diag_block),
+        pin(flux_block),
+        pin(cell_list.reshape(BLOCKS, BLK)),
         block_count,
-        helper_of.reshape(1, BLOCKS),
-        flash_inverse.reshape(BLOCKS, NC, NC, BLK),
-        flash_coupling.reshape(BLOCKS, NC, NC, BLK),
-        phase_state.reshape(BLOCKS, NC, BLK),
+        pin(helper_of.reshape(1, BLOCKS)),
+        pin(flash_inverse.reshape(BLOCKS, NC, NC, BLK)),
+        pin(flash_coupling.reshape(BLOCKS, NC, NC, BLK)),
+        pin(phase_state.reshape(BLOCKS, NC, BLK)),
     )
     return adjoint.reshape(cotangent.shape), grad
 

time: 90.9 us -> 82 us (0.902)
  Pallas kernels: 86.1 us -> 78.7 us
  local copies, waits for them, and re-layouts: 3.32 us -> 1.74 us
    pallas_call x1, Pallas kernels: 86.1 us -> 78.7 us  [shards(): pl.pallas_call(kernel, out_shape=(pltpu.VMEM((FIELDS * CY, CX), F32), plt...]
    unnamed x4 -> x2, local copies, waits for them, and re-layouts: 3.32 us -> 1.74 us
where the time goes in v2:
time: 82 us; the launch traced here: 81.7 us
  Pallas kernels  78.7 us (96%)
  local copies, waits for them, and re-layouts  1.74 us (2%)
  between operations  1.29 us (2%)
    pallas_call x1, Pallas kernels, shards(): pl.pallas_call(kernel, out_shape=(pltpu.VMEM((FIELDS * CY, CX), F32), plt...  78.7 us
    unnamed x2, local copies, waits for them, and re-layouts  1.74 us

profile of v2, /device:TPU:1, one launch (start us, length us, event | category | flops | bytes accessed | tf_op | source)
XLA Modules:
  0.0 81.7 jit_solution(13756820618446338130)
XLA Ops:
  1.3 78.7 %shard_map.122 = (f32[3072,128]{1,0:T(8,128)S(1)}, f32[8,8]{1,0:T(8,128)S(1)}) custom-call(f32[3072,128]{1,0:T(8,128)} %bitcast.11, f32[384,128]{1,0:T(8,128)} %bitcast.13, s32[64,128]{1,0:T(8,128)} %mask_h.1, bf16[6,8,8,64,128]{4,3,2,1,0:T(8,128)(2,1)} %diag_h.1, bf16[6,8,8,64,128]{4,3,2,1,0:T(8,128)(2,1)} %flux_h.1, s32[128,128]{1,0:T(8,128)} %bitcast.14, ...), custom_call_target="tpu_custom_call" | custom-call | tf_op jit(solution)/shard_map/pallas_call | solution.py:493
  80.0 1.1 %copy.15 = f32[6,8,64,128]{3,2,1,0:T(8,128)} copy(f32[6,8,64,128]{3,2,1,0:T(8,128)S(1)} %bitcast.8) | data formatting | bytes 3145728
  81.1 0.6 copy.16

commit v3 on v2

--- a/solution.py
+++ b/solution.py
@@ -18,9 +18,10 @@
 WX, WY = 8, 16
 DEVICES = WX * WY
 BLOCKS, BLK = 128, 128
-NB = 8
+NB = 16
+SUB = 8
 CHUNKS = BLOCKS // NB
-DELAY = 5
+DELAY = 4
 ROWS = 16
 
 
@@ -28,7 +29,7 @@
     cot_h, perm_h, mask_h, diag_h, flux_h, cells_h, count_ref, helper_h, inv_h, coup_h, phase_h,
     out_v, grad_ref,
     cot_v, perm_v, mask_v, cells_ref, helper_ref, diag_v, flux_v, inv_v, coup_v, phase_v,
-    w_v, k_v, t_v, f16_v, s2_v, code_v, y_v, oh_v, lhs_v,
+    w_v, west_v, east_v, k_v, t_v, f16_v, s2_v, code_v, y_v, oh_v, lhs_v,
     ps, rb, cs, cr, g_v, gt, ga, gt2, gb,
     hx_s, hx_r, hy_s, hy_r,
     load_sem, blk_sem, fl_sem,
@@ -40,6 +41,16 @@
 
     def device(linear):
         return (lax.div(linear, WY), lax.rem(linear, WY))
+
+    barrier = pltpu.get_barrier_semaphore()
+
+    def greet(step, carry):
+        pl.semaphore_signal(
+            barrier, inc=1, device_id=device(lax.rem(me + step, DEVICES)), device_id_type=MESH
+        )
+        return carry
+
+    lax.fori_loop(1, DEVICES, greet, 0)
 
     loads = [
         pltpu.make_async_copy(cot_h, cot_v, load_sem.at[0]),
@@ -68,15 +79,181 @@
     for copy in flash_loads:
         copy.start()
 
-    barrier = pltpu.get_barrier_semaphore()
-
-    def greet(step, carry):
-        pl.semaphore_signal(
-            barrier, inc=1, device_id=device(lax.rem(me + step, DEVICES)), device_id_type=MESH
-        )
-        return carry
-
-    lax.fori_loop(1, DEVICES, greet, 0)
+    w_v[pl.ds(0, NC * PAD), :] = jnp.zeros((NC * PAD, CX), F32)
+    w_v[pl.ds((FIELDS + NC) * PAD, NC * PAD), :] = jnp.zeros((NC * PAD, CX), F32)
+    k_v[pl.ds(0, PAD), :] = jnp.zeros((PAD, CX), F32)
+    k_v[pl.ds((LAYERS + 1) * PAD, PAD), :] = jnp.zeros((PAD, CX), F32)
+
+    for copy in loads:
+        copy.wait()
+
+    lane_y = lax.broadcasted_iota(jnp.int32, (CY, CX), 1)
+    hole = mask_v[...].astype(F32)
+    keep = 1.0 - hole
+
+    def field(q):
+        return pl.ds(pl.multiple_of(q * CY, CY), CY)
+
+    def pack_edges(q, value, carry):
+        right, left = carry
+        turned = pltpu.roll(value, 2 * q + 2, axis=1)
+        right = jnp.where(lane_y == 2 * q + 1, turned, right)
+        left = jnp.where(lane_y == 2 * q + 2, turned, left)
+        return right, left
+
+    def mask_fields(source, which, start):
+        def step(q, carry):
+            value = source[field(q), :] * keep
+            w_v[pl.ds(pl.multiple_of((q + NC) * PAD + 8, 8), CY), :] = value
+            return pack_edges(q, value, carry)
+
+        right, left = lax.fori_loop(0, FIELDS, step, start, unroll=8)
+        hx_s[which, 0] = pltpu.roll(left, CX - 2, axis=1)
+        hx_s[which, 1] = right
+        for layer in range(LAYERS):
+            base = (layer + 1) * NC * PAD + 8
+            hy_s[which, 0, pl.ds(layer * NC, NC), :] = w_v[pl.ds(base, NC, stride=PAD), :]
+            hy_s[which, 1, pl.ds(layer * NC, NC), :] = w_v[pl.ds(base + CY - 1, NC, stride=PAD), :]
+
+    def halo_copies(which):
+        east = (lax.rem(gx + 1, WX), gy)
+        west = (lax.rem(gx + WX - 1, WX), gy)
+        south = (gx, lax.rem(gy + 1, WY))
+        north = (gx, lax.rem(gy + WY - 1, WY))
+        plan = (
+            (hx_s.at[which, 1], hx_r.at[which, 0], east),
+            (hx_s.at[which, 0], hx_r.at[which, 1], west),
+            (hy_s.at[which, 1], hy_r.at[which, 0], south),
+            (hy_s.at[which, 0], hy_r.at[which, 1], north),
+        )
+        return [
+            pltpu.make_async_remote_copy(
+                src_ref=source,
+                dst_ref=target_ref,
+                send_sem=halo_send.at[which, i],
+                recv_sem=halo_recv.at[which, i],
+                device_id=where,
+                device_id_type=MESH,
+            )
+            for i, (source, target_ref, where) in enumerate(plan)
+        ]
+
+    def edge_columns(which):
+        odd = lax.rem(lane_y, 2) == 1
+        from_west = jnp.where(gx > 0, hx_r[which, 0], 0.0)
+        from_east = jnp.where(gx < WX - 1, hx_r[which, 1], 0.0)
+        hx_r[which, 0] = jnp.where(odd, from_west, from_east)
+
+    def edge_rows(which):
+        for layer in range(LAYERS):
+            base = (layer + 1) * NC * PAD
+            rows = pl.ds(layer * NC, NC)
+            w_v[pl.ds(base + 7, NC, stride=PAD), :] = jnp.where(gy > 0, hy_r[which, 0, rows, :], 0.0)
+            w_v[pl.ds(base + 8 + CY, NC, stride=PAD), :] = jnp.where(
+                gy < WY - 1, hy_r[which, 1, rows, :], 0.0
+            )
+
+    zero_edge = jnp.zeros((CY, CX), F32)
+    start = (zero_edge, zero_edge)
+    for layer in range(LAYERS):
+        value = perm_v[pl.ds(layer * CY, CY), :]
+        k_v[pl.ds((layer + 1) * PAD + 8, CY), :] = value
+        start = pack_edges(FIELDS + layer, value, start)
+    mask_fields(cot_v, 0, start)
+    for layer in range(LAYERS):
+        base = (layer + 1) * PAD + 8
+        hy_s[0, 0, pl.ds(FIELDS + layer, 1), :] = k_v[pl.ds(base, 1), :]
+        hy_s[0, 1, pl.ds(FIELDS + layer, 1), :] = k_v[pl.ds(base + CY - 1, 1), :]
+
+    pl.semaphore_wait(barrier, DEVICES - 1)
+    first_halo = halo_copies(0)
+    for copy in first_halo:
+        copy.start()
+
+    def beside_x(edges, q, lane, west, east):
+        turned = pltpu.roll(edges, CX - 1 - 2 * q, axis=1)
+        return jnp.where(lane == 0, turned, west), jnp.where(lane == CX - 1, turned, east)
+
+    def make_weights(layer, carry):
+        base = pl.multiple_of((layer + 1) * PAD, 8)
+        centre = k_v[pl.ds(base + 8, CY), :]
+        west, east = beside_x(
+            hx_r[0, 0],
+            FIELDS + layer,
+            lane_y,
+            pltpu.roll(centre, 1, axis=1),
+            pltpu.roll(centre, CX - 1, axis=1),
+        )
+        others = (
+            k_v[pl.ds(base + 8 + PAD, CY), :],
+            k_v[pl.ds(base + 8 - PAD, CY), :],
+            k_v[pl.ds(base + 9, CY), :],
+            k_v[pl.ds(base + 7, CY), :],
+            east,
+            west,
+        )
+        for i, other in enumerate(others):
+            t_v[i, field(layer), :] = 2.0 * centre * other / (centre + other)
+        return carry
+
+    lane_r = lax.broadcasted_iota(jnp.int32, (ROWS, CX), 1)
+
+    def part_rows(layer, c, r0):
+        return pl.ds(pl.multiple_of((layer * NC + c) * CY + r0, ROWS), ROWS)
+
+    def diag_pass(layer, source, held):
+        for r0 in range(0, CY, ROWS):
+            well = mask_v[pl.ds(r0, ROWS), :].astype(F32)
+            acc = [well * source[part_rows(layer, c, r0), :] for c in range(NC)]
+            for r in range(NC):
+                base = pl.multiple_of((layer + 1) * (NC * PAD) + (r * PAD + 8 + r0), 8)
+                own = w_v[pl.ds(base, ROWS), :]
+                west_v[part_rows(layer, r, r0), :] = pltpu.roll(own, 1, axis=1)
+                east_v[part_rows(layer, r, r0), :] = pltpu.roll(own, CX - 1, axis=1)
+                for c in range(NC):
+                    acc[c] = acc[c] + diag_v[layer, r, c, pl.ds(r0, ROWS), :].astype(F32) * own
+            for c in range(NC):
+                held[part_rows(layer, c, r0), :] = acc[c]
+
+    def flux_pass(layer, which, held, put):
+        for r0 in range(0, CY, ROWS):
+            rows = pl.ds(pl.multiple_of(layer * CY + r0, ROWS), ROWS)
+            weights = [t_v[i, rows, :] for i in range(6)]
+            edges = hx_r[which, 0, pl.ds(r0, ROWS), :]
+            acc = [held[part_rows(layer, c, r0), :] for c in range(NC)]
+            for r in range(NC):
+                base = pl.multiple_of((layer + 1) * (NC * PAD) + (r * PAD + 8 + r0), 8)
+                here = part_rows(layer, r, r0)
+                west, east = beside_x(
+                    edges, layer * NC + r, lane_r, west_v[here, :], east_v[here, :]
+                )
+                total = weights[0] * w_v[pl.ds(base + NC * PAD, ROWS), :]
+                total = total + weights[1] * w_v[pl.ds(base - NC * PAD, ROWS), :]
+                total = total + weights[2] * w_v[pl.ds(base + 1, ROWS), :]
+                total = total + weights[3] * w_v[pl.ds(base - 1, ROWS), :]
+                total = total + weights[4] * east
+                total = total + weights[5] * west
+                for c in range(NC):
+                    acc[c] = acc[c] - flux_v[layer, r, c, pl.ds(r0, ROWS), :].astype(F32) * total
+            for c in range(NC):
+                put(layer, c, r0, acc[c])
+
+    def put_first(layer, c, r0, value):
+        lanes = pl.ds(pl.multiple_of(layer * CX, CX), CX)
+        f16_v[pl.ds(c * CY + r0, ROWS), lanes] = value.astype(BF16)
+        s2_v[part_rows(layer, c, r0), :] = value
+
+    def first_diag(layer, carry):
+        block_copy(0, layer).wait()
+        diag_pass(layer, cot_v, s2_v)
+        return carry
+
+    def first_flux(layer, carry):
+        block_copy(1, layer).wait()
+        flux_pass(layer, 0, s2_v, put_first)
+        return carry
+
+    lax.fori_loop(0, LAYERS, first_diag, 0)
 
     for copy in table_loads:
         copy.wait()
@@ -94,174 +271,6 @@
     )
     y_v[...] = jnp.dot(choose, cell_y, preferred_element_type=F32)
 
-    w_v[pl.ds(0, NC * PAD), :] = jnp.zeros((NC * PAD, CX), F32)
-    w_v[pl.ds((FIELDS + NC) * PAD, NC * PAD), :] = jnp.zeros((NC * PAD, CX), F32)
-    k_v[pl.ds(0, PAD), :] = jnp.zeros((PAD, CX), F32)
-    k_v[pl.ds((LAYERS + 1) * PAD, PAD), :] = jnp.zeros((PAD, CX), F32)
-
-    for copy in loads:
-        copy.wait()
-
-    lane_y = lax.broadcasted_iota(jnp.int32, (CY, CX), 1)
-    hole = mask_v[...].astype(F32)
-    keep = 1.0 - hole
-
-    def field(q):
-        return pl.ds(pl.multiple_of(q * CY, CY), CY)
-
-    def pack_edges(q, value, carry):
-        right, left = carry
-        turned = pltpu.roll(value, 2 * q + 2, axis=1)
-        right = jnp.where(lane_y == 2 * q + 1, turned, right)
-        left = jnp.where(lane_y == 2 * q + 2, turned, left)
-        return right, left
-
-    def mask_fields(source, which, start):
-        def step(q, carry):
-            value = source[field(q), :] * keep
-            w_v[pl.ds(pl.multiple_of((q + NC) * PAD + 8, 8), CY), :] = value
-            return pack_edges(q, value, carry)
-
-        right, left = lax.fori_loop(0, FIELDS, step, start, unroll=2)
-        hx_s[which, 0] = left
-        hx_s[which, 1] = right
-        for layer in range(LAYERS):
-            base = (layer + 1) * NC * PAD + 8
-            hy_s[which, 0, pl.ds(layer * NC, NC), :] = w_v[pl.ds(base, NC, stride=PAD), :]
-            hy_s[which, 1, pl.ds(layer * NC, NC), :] = w_v[pl.ds(base + CY - 1, NC, stride=PAD), :]
-
-    def halo_copies(which):
-        east = (lax.rem(gx + 1, WX), gy)
-        west = (lax.rem(gx + WX - 1, WX), gy)
-        south = (gx, lax.rem(gy + 1, WY))
-        north = (gx, lax.rem(gy + WY - 1, WY))
-        plan = (
-            (hx_s.at[which, 1], hx_r.at[which, 0], east),
-            (hx_s.at[which, 0], hx_r.at[which, 1], west),
-            (hy_s.at[which, 1], hy_r.at[which, 0], south),
-            (hy_s.at[which, 0], hy_r.at[which, 1], north),
-        )
-        return [
-            pltpu.make_async_remote_copy(
-                src_ref=source,
-                dst_ref=target_ref,
-                send_sem=halo_send.at[which, i],
-                recv_sem=halo_recv.at[which, i],
-                device_id=where,
-                device_id_type=MESH,
-            )
-            for i, (source, target_ref, where) in enumerate(plan)
-        ]
-
-    def edge_columns(which):
-        odd = lax.rem(lane_y, 2) == 1
-        from_west = jnp.where(gx > 0, hx_r[which, 0], 0.0)
-        from_east = jnp.where(gx < WX - 1, hx_r[which, 1], 0.0)
-        hx_r[which, 0] = jnp.where(odd, from_west, from_east)
-
-    def edge_rows(which):
-        for layer in range(LAYERS):
-            base = (layer + 1) * NC * PAD
-            rows = pl.ds(layer * NC, NC)
-            w_v[pl.ds(base + 7, NC, stride=PAD), :] = jnp.where(gy > 0, hy_r[which, 0, rows, :], 0.0)
-            w_v[pl.ds(base + 8 + CY, NC, stride=PAD), :] = jnp.where(
-                gy < WY - 1, hy_r[which, 1, rows, :], 0.0
-            )
-
-    zero_edge = jnp.zeros((CY, CX), F32)
-    start = (zero_edge, zero_edge)
-    for layer in range(LAYERS):
-        value = perm_v[pl.ds(layer * CY, CY), :]
-        k_v[pl.ds((layer + 1) * PAD + 8, CY), :] = value
-        start = pack_edges(FIELDS + layer, value, start)
-    mask_fields(cot_v, 0, start)
-    for layer in range(LAYERS):
-        base = (layer + 1) * PAD + 8
-        hy_s[0, 0, pl.ds(FIELDS + layer, 1), :] = k_v[pl.ds(base, 1), :]
-        hy_s[0, 1, pl.ds(FIELDS + layer, 1), :] = k_v[pl.ds(base + CY - 1, 1), :]
-
-    pl.semaphore_wait(barrier, DEVICES - 1)
-    first_halo = halo_copies(0)
-    for copy in first_halo:
-        copy.start()
-
-    def beside_x(value, edges, shift, lane):
-        turned = pltpu.roll(edges, shift, axis=1)
-        west = pltpu.roll(jnp.where(lane == CX - 1, turned, value), 1, axis=1)
-        east = pltpu.roll(jnp.where(lane == 0, turned, value), CX - 1, axis=1)
-        return west, east
-
-    def make_weights(layer, carry):
-        base = pl.multiple_of((layer + 1) * PAD, 8)
-        centre = k_v[pl.ds(base + 8, CY), :]
-        west, east = beside_x(centre, hx_r[0, 0], CX - 2 * (FIELDS + layer) - 2, lane_y)
-        others = (
-            k_v[pl.ds(base + 8 + PAD, CY), :],
-            k_v[pl.ds(base + 8 - PAD, CY), :],
-            k_v[pl.ds(base + 9, CY), :],
-            k_v[pl.ds(base + 7, CY), :],
-            east,
-            west,
-        )
-        for i, other in enumerate(others):
-            t_v[i, field(layer), :] = 2.0 * centre * other / (centre + other)
-        return carry
-
-    lane_r = lax.broadcasted_iota(jnp.int32, (ROWS, CX), 1)
-
-    def part_rows(layer, c, r0):
-        return pl.ds(pl.multiple_of((layer * NC + c) * CY + r0, ROWS), ROWS)
-
-    def diag_pass(layer, source, held):
-        for r0 in range(0, CY, ROWS):
-            well = mask_v[pl.ds(r0, ROWS), :].astype(F32)
-            acc = [well * source[part_rows(layer, c, r0), :] for c in range(NC)]
-            for r in range(NC):
-                base = pl.multiple_of((layer + 1) * (NC * PAD) + (r * PAD + 8 + r0), 8)
-                own = w_v[pl.ds(base, ROWS), :]
-                for c in range(NC):
-                    acc[c] = acc[c] + diag_v[layer, r, c, pl.ds(r0, ROWS), :].astype(F32) * own
-            for c in range(NC):
-                held[part_rows(layer, c, r0), :] = acc[c]
-
-    def flux_pass(layer, which, held, put):
-        for r0 in range(0, CY, ROWS):
-            rows = pl.ds(pl.multiple_of(layer * CY + r0, ROWS), ROWS)
-            weights = [t_v[i, rows, :] for i in range(6)]
-            edges = hx_r[which, 0, pl.ds(r0, ROWS), :]
-            acc = [held[part_rows(layer, c, r0), :] for c in range(NC)]
-            for r in range(NC):
-                base = pl.multiple_of((layer + 1) * (NC * PAD) + (r * PAD + 8 + r0), 8)
-                value = w_v[pl.ds(base, ROWS), :]
-                west, east = beside_x(value, edges, CX - 2 * (layer * NC + r) - 2, lane_r)
-                total = weights[0] * w_v[pl.ds(base + NC * PAD, ROWS), :]
-                total = total + weights[1] * w_v[pl.ds(base - NC * PAD, ROWS), :]
-                total = total + weights[2] * w_v[pl.ds(base + 1, ROWS), :]
-                total = total + weights[3] * w_v[pl.ds(base - 1, ROWS), :]
-                total = total + weights[4] * east
-                total = total + weights[5] * west
-                for c in range(NC):
-                    acc[c] = acc[c] - flux_v[layer, r, c, pl.ds(r0, ROWS), :].astype(F32) * total
-            for c in range(NC):
-                put(layer, c, r0, acc[c])
-
-    def put_first(layer, c, r0, value):
-        lanes = pl.ds(pl.multiple_of(layer * CX, CX), CX)
-        f16_v[pl.ds(c * CY + r0, ROWS), lanes] = value.astype(BF16)
-        s2_v[part_rows(layer, c, r0), :] = value
-
-    def first_diag(layer, carry):
-        block_copy(0, layer).wait()
-        diag_pass(layer, cot_v, s2_v)
-        return carry
-
-    def first_flux(layer, carry):
-        block_copy(1, layer).wait()
-        flux_pass(layer, 0, s2_v, put_first)
-        return carry
-
-    lax.fori_loop(0, LAYERS, first_diag, 0)
-
     for copy in first_halo:
         copy.wait_recv()
     edge_columns(0)
@@ -279,14 +288,17 @@
 
     iota_x = lax.broadcasted_iota(jnp.int32, (CX, BLK), 0).astype(F32).astype(BF16)
     iota_y = lax.broadcasted_iota(jnp.int32, (CY, BLK), 0).astype(F32)
+    iota_y16 = iota_y.astype(BF16)
     one16 = jnp.ones((CX, BLK), BF16)
     zero16 = jnp.zeros((CX, BLK), BF16)
 
-    def one_hot(p, b):
-        code = code_v[pl.ds(p, 1), :]
+    def one_hot(chunk, b):
+        code = code_v[pl.ds(chunk * NB + b, 1), :]
         for layer in range(LAYERS):
             own_x = jnp.broadcast_to((code - float(layer * CX)).astype(BF16), (CX, BLK))
-            oh_v[pl.ds(layer * CX, CX), pl.ds(b * BLK, BLK)] = jnp.where(own_x == iota_x, one16, zero16)
+            oh_v[chunk, pl.ds(layer * CX, CX), pl.ds(b * BLK, BLK)] = jnp.where(
+                own_x == iota_x, one16, zero16
+            )
 
     def send_chunk(buf, to, chunk, sign, send, recv):
         for b in range(NB):
@@ -323,17 +335,22 @@
         )
 
     def gather(chunk):
-        for b in range(NB):
-            one_hot(chunk * NB + b, b)
-        wide = jnp.dot(f16_v[...], oh_v[...], preferred_element_type=F32)
-        for b in range(NB):
-            p = chunk * NB + b
-            hit = jnp.broadcast_to(y_v[pl.ds(p, 1), :], (CY, BLK)) == iota_y
-            found = []
-            for c in range(NC):
-                piece = wide[c * CY : (c + 1) * CY, b * BLK : (b + 1) * BLK]
-                found.append(jnp.sum(jnp.where(hit, piece, 0.0), axis=0, keepdims=True))
-            ps[p] = jnp.concatenate(found, axis=0).astype(BF16)
+        for first in range(0, NB, SUB):
+            for b in range(first, first + SUB):
+                one_hot(chunk, b)
+            wide = jnp.dot(
+                f16_v[...],
+                oh_v[chunk, :, first * BLK : (first + SUB) * BLK],
+                preferred_element_type=F32,
+            )
+            for b in range(SUB):
+                p = chunk * NB + first + b
+                hit = jnp.broadcast_to(y_v[pl.ds(p, 1), :], (CY, BLK)) == iota_y
+                found = []
+                for c in range(NC):
+                    piece = wide[c * CY : (c + 1) * CY, b * BLK : (b + 1) * BLK]
+                    found.append(jnp.sum(jnp.where(hit, piece, 0.0), axis=0, keepdims=True))
+                ps[p] = jnp.concatenate(found, axis=0).astype(BF16)
 
     def flash(chunk):
         total = g_v[...]
@@ -351,15 +368,14 @@
     def scatter(chunk):
         for b in range(NB):
             p = chunk * NB + b
-            one_hot(p, b)
-            hit = jnp.broadcast_to(y_v[pl.ds(p, 1), :], (CY, BLK)) == iota_y
-            change = cr[p].astype(F32)
+            hit = jnp.broadcast_to(y_v[pl.ds(p, 1), :].astype(BF16), (CY, BLK)) == iota_y16
+            change = cr[p]
             for c in range(NC):
                 lhs_v[pl.ds(c * CY, CY), pl.ds(b * BLK, BLK)] = jnp.where(
-                    hit, jnp.broadcast_to(change[c : c + 1], (CY, BLK)), 0.0
-                ).astype(BF16)
+                    hit, jnp.broadcast_to(change[c : c + 1], (CY, BLK)), zero16[:CY]
+                )
         added = lax.dot_general(
-            lhs_v[...], oh_v[...], (((1,), (1,)), ((), ())), preferred_element_type=F32
+            lhs_v[...], oh_v[chunk], (((1,), (1,)), ((), ())), preferred_element_type=F32
         )
         for layer in range(LAYERS):
             rows = pl.ds(layer * NC * CY, NC * CY)
@@ -510,13 +526,15 @@
             pltpu.VMEM((BLOCKS, NC, NC, BLK), BF16),
             pltpu.VMEM((BLOCKS, NC, BLK), BF16),
             pltpu.VMEM(((FIELDS + 2 * NC) * PAD, CX), F32),
+            pltpu.VMEM((FIELDS * CY, CX), F32),
+            pltpu.VMEM((FIELDS * CY, CX), F32),
             pltpu.VMEM(((LAYERS + 2) * PAD, CX), F32),
             pltpu.VMEM((6, LAYERS * CY, CX), F32),
             pltpu.VMEM((NC * CY, LAYERS * CX), BF16),
             pltpu.VMEM((FIELDS * CY, CX), F32),
             pltpu.VMEM((BLOCKS, BLK), F32),
             pltpu.VMEM((BLOCKS, BLK), F32),
-            pltpu.VMEM((LAYERS * CX, NB * BLK), BF16),
+            pltpu.VMEM((CHUNKS, LAYERS * CX, NB * BLK), BF16),
             pltpu.VMEM((NC * CY, NB * BLK), BF16),
             pltpu.VMEM((BLOCKS, NC, BLK), BF16),
             pltpu.VMEM((BLOCKS, NC, BLK), BF16),
@@ -544,7 +562,7 @@
             dma((2,)),
         ],
         compiler_params=pltpu.CompilerParams(
-            collective_id=0, has_side_effects=True, vmem_limit_bytes=50 << 20
+            collective_id=0, has_side_effects=True, vmem_limit_bytes=60 << 20
         ),
     )(
         pin(cotangent.reshape(FIELDS * CY, CX)),

time: 82 us -> 66.9 us (0.82)
  Pallas kernels: 78.7 us -> 63.8 us
    pallas_call x1, Pallas kernels: 78.7 us -> 63.8 us  [shards(): pl.pallas_call(kernel, out_shape=(pltpu.VMEM((FIELDS * CY, CX), F32), plt...]
where the time goes in v3:
time: 66.9 us; the launch traced here: 66.8 us
  Pallas kernels  63.8 us (95%)
  local copies, waits for them, and re-layouts  1.74 us (3%)
  between operations  1.29 us (2%)
    pallas_call x1, Pallas kernels, shards(): pl.pallas_call(kernel, out_shape=(pltpu.VMEM((FIELDS * CY, CX), F32), plt...  63.8 us
    unnamed x2, local copies, waits for them, and re-layouts  1.74 us

profile of v3, /device:TPU:1, one launch (start us, length us, event | category | flops | bytes accessed | tf_op | source)
XLA Modules:
  0.0 66.8 jit_solution(3951889232316185731)
XLA Ops:
  1.3 63.8 %shard_map.122 = (f32[3072,128]{1,0:T(8,128)S(1)}, f32[8,8]{1,0:T(8,128)S(1)}) custom-call(f32[3072,128]{1,0:T(8,128)} %bitcast.11, f32[384,128]{1,0:T(8,128)} %bitcast.13, s32[64,128]{1,0:T(8,128)} %mask_h.1, bf16[6,8,8,64,128]{4,3,2,1,0:T(8,128)(2,1)} %diag_h.1, bf16[6,8,8,64,128]{4,3,2,1,0:T(8,128)(2,1)} %flux_h.1, s32[128,128]{1,0:T(8,128)} %bitcast.14, ...), custom_call_target="tpu_custom_call" | custom-call | tf_op jit(solution)/shard_map/pallas_call | solution.py:509
  65.1 1.1 %copy.15 = f32[6,8,64,128]{3,2,1,0:T(8,128)} copy(f32[6,8,64,128]{3,2,1,0:T(8,128)S(1)} %bitcast.8) | data formatting | bytes 3145728
  66.2 0.6 copy.16

commit v4 on v3

--- a/solution.py
+++ b/solution.py
@@ -30,9 +30,9 @@
     out_v, grad_ref,
     cot_v, perm_v, mask_v, cells_ref, helper_ref, diag_v, flux_v, inv_v, coup_v, phase_v,
     w_v, west_v, east_v, k_v, t_v, f16_v, s2_v, code_v, y_v, oh_v, lhs_v,
-    ps, rb, cs, cr, g_v, gt, ga, gt2, gb,
+    ps, rb, cs, cr, row_v, g_v, gt, ga, gt2, gb,
     hx_s, hx_r, hy_s, hy_r,
-    load_sem, blk_sem, fl_sem,
+    load_sem, cot_sem, blk_sem, fl_sem,
     halo_send, halo_recv, ps_send, ps_recv, cs_send, cs_recv, g_send, g_recv,
 ):
     gx = lax.axis_index("gx")
@@ -42,18 +42,11 @@
     def device(linear):
         return (lax.div(linear, WY), lax.rem(linear, WY))
 
-    barrier = pltpu.get_barrier_semaphore()
-
-    def greet(step, carry):
-        pl.semaphore_signal(
-            barrier, inc=1, device_id=device(lax.rem(me + step, DEVICES)), device_id_type=MESH
-        )
-        return carry
-
-    lax.fori_loop(1, DEVICES, greet, 0)
+    def cot_copy(layer):
+        rows = pl.ds(pl.multiple_of(layer * NC * CY, NC * CY), NC * CY)
+        return pltpu.make_async_copy(cot_h.at[rows], cot_v.at[rows], cot_sem.at[layer])
 
     loads = [
-        pltpu.make_async_copy(cot_h, cot_v, load_sem.at[0]),
         pltpu.make_async_copy(perm_h, perm_v, load_sem.at[1]),
         pltpu.make_async_copy(mask_h, mask_v, load_sem.at[2]),
     ]
@@ -61,7 +54,22 @@
         pltpu.make_async_copy(cells_h, cells_ref, load_sem.at[3]),
         pltpu.make_async_copy(helper_h, helper_ref, load_sem.at[4]),
     ]
-    for copy in loads + table_loads:
+    for copy in loads:
+        copy.start()
+    for layer in range(LAYERS):
+        cot_copy(layer).start()
+
+    barrier = pltpu.get_barrier_semaphore()
+
+    def greet(step, carry):
+        pl.semaphore_signal(
+            barrier, inc=1, device_id=device(lax.rem(me + step, DEVICES)), device_id_type=MESH
+        )
+        return carry
+
+    lax.fori_loop(1, DEVICES, greet, 0)
+
+    for copy in table_loads:
         copy.start()
 
     def block_copy(which, layer):
@@ -102,12 +110,17 @@
         return right, left
 
     def mask_fields(source, which, start):
-        def step(q, carry):
-            value = source[field(q), :] * keep
-            w_v[pl.ds(pl.multiple_of((q + NC) * PAD + 8, 8), CY), :] = value
-            return pack_edges(q, value, carry)
-
-        right, left = lax.fori_loop(0, FIELDS, step, start, unroll=8)
+        def step(layer, carry):
+            if which == 0:
+                cot_copy(layer).wait()
+            for c in range(NC):
+                q = layer * NC + c
+                value = source[field(q), :] * keep
+                w_v[pl.ds(pl.multiple_of((q + NC) * PAD + 8, 8), CY), :] = value
+                carry = pack_edges(q, value, carry)
+            return carry
+
+        right, left = lax.fori_loop(0, LAYERS, step, start)
         hx_s[which, 0] = pltpu.roll(left, CX - 2, axis=1)
         hx_s[which, 1] = right
         for layer in range(LAYERS):
@@ -352,18 +365,30 @@
                     found.append(jnp.sum(jnp.where(hit, piece, 0.0), axis=0, keepdims=True))
                 ps[p] = jnp.concatenate(found, axis=0).astype(BF16)
 
+    def spread(value, b, i):
+        row_v[b, i] = value
+        return [jnp.broadcast_to(row_v[b, i, pl.ds(r, 1), :], (NC, BLK)) for r in range(NC)]
+
+    def weighted(matrix, rows):
+        total = matrix[0] * rows[0]
+        for r in range(1, NC):
+            total = total + matrix[r] * rows[r]
+        return total
+
     def flash(chunk):
-        total = g_v[...]
+        totals = [g_v[j] for j in range(NC)]
         for b in range(NB):
             p = chunk * NB + b
             source = lax.rem(me - (p + 1) + DEVICES, DEVICES)
-            chosen = rb[p].astype(F32)
-            multiplier = jnp.sum(inv_v[source].astype(F32) * chosen[:, None, :], axis=0)
-            change = -jnp.sum(coup_v[source].astype(F32) * multiplier[:, None, :], axis=0)
+            multiplier = weighted(inv_v[source].astype(F32), spread(rb[p].astype(F32), b, 0))
+            change = -weighted(coup_v[source].astype(F32), spread(multiplier, b, 1))
+            cs[p] = change.astype(BF16)
             state = phase_v[source].astype(F32)
-            total = total + (multiplier * state)[None] * state[:, None, :]
-            cs[p] = change.astype(BF16)
-        g_v[...] = total
+            term = multiplier * state
+            for j, row in enumerate(spread(state, b, 2)):
+                totals[j] = totals[j] + term * row
+        for j in range(NC):
+            g_v[j] = totals[j]
 
     def scatter(chunk):
         for b in range(NB):
@@ -432,6 +457,11 @@
 
     loop(CHUNKS + DELAY, 2 * CHUNKS, scatters=CHUNKS)
 
+    mask_fields(s2_v, 1, (zero_edge, zero_edge))
+    second_halo = halo_copies(1)
+    for copy in second_halo:
+        copy.start()
+
     some = ga.at[pl.ds(0, WX - 1)]
     grad_copy(some, some, (lax.rem(gx + 1, WX), gy), 0).wait_recv()
     part = ga[0]
@@ -446,10 +476,6 @@
 
     lax.fori_loop(1, WY, send_y, 0)
 
-    mask_fields(s2_v, 1, (zero_edge, zero_edge))
-    second_halo = halo_copies(1)
-    for copy in second_halo:
-        copy.start()
 
     def second_diag(layer, carry):
         diag_pass(layer, s2_v, out_v)
@@ -540,6 +566,7 @@
             pltpu.VMEM((BLOCKS, NC, BLK), BF16),
             pltpu.VMEM((BLOCKS, NC, BLK), BF16),
             pltpu.VMEM((BLOCKS, NC, BLK), BF16),
+            pltpu.VMEM((NB, 3, NC, BLK), F32),
             pltpu.VMEM((NC, NC, BLK), F32),
             pltpu.VMEM((NC, CX), F32),
             pltpu.VMEM((WX, NC, CX), F32),
@@ -550,6 +577,7 @@
             pltpu.VMEM((2, 2, 56, CX), F32),
             pltpu.VMEM((2, 2, 56, CX), F32),
             dma((5,)),
+            dma((LAYERS,)),
             dma((2, LAYERS)),
             dma((3,)),
             dma((2, 4)),

time: 66.9 us -> 65.3 us (0.976)
  Pallas kernels: 63.8 us -> 61.7 us
    pallas_call x1, Pallas kernels: 63.8 us -> 61.7 us  [shards(): pl.pallas_call(kernel, out_shape=(pltpu.VMEM((FIELDS * CY, CX), F32), plt...]
where the time goes in v4:
time: 65.3 us; the launch traced here: 64.7 us
  Pallas kernels  61.7 us (94%)
  local copies, waits for them, and re-layouts  1.74 us (3%)
  between operations  1.29 us (2%)
    pallas_call x1, Pallas kernels, shards(): pl.pallas_call(kernel, out_shape=(pltpu.VMEM((FIELDS * CY, CX), F32), plt...  61.7 us
    unnamed x2, local copies, waits for them, and re-layouts  1.74 us

profile of v4, /device:TPU:1, one launch (start us, length us, event | category | flops | bytes accessed | tf_op | source)
XLA Modules:
  0.0 64.7 jit_solution(6615016643901128218)
XLA Ops:
  1.3 61.7 %shard_map.122 = (f32[3072,128]{1,0:T(8,128)S(1)}, f32[8,8]{1,0:T(8,128)S(1)}) custom-call(f32[3072,128]{1,0:T(8,128)} %bitcast.11, f32[384,128]{1,0:T(8,128)} %bitcast.13, s32[64,128]{1,0:T(8,128)} %mask_h.1, bf16[6,8,8,64,128]{4,3,2,1,0:T(8,128)(2,1)} %diag_h.1, bf16[6,8,8,64,128]{4,3,2,1,0:T(8,128)(2,1)} %flux_h.1, s32[128,128]{1,0:T(8,128)} %bitcast.14, ...), custom_call_target="tpu_custom_call" | custom-call | tf_op jit(solution)/shard_map/pallas_call | solution.py:535
  63.0 1.1 %copy.15 = f32[6,8,64,128]{3,2,1,0:T(8,128)} copy(f32[6,8,64,128]{3,2,1,0:T(8,128)S(1)} %bitcast.8) | data formatting | bytes 3145728
  64.1 0.6 copy.16

commit v5 on v4

--- a/solution.py
+++ b/solution.py
@@ -309,7 +309,7 @@
         code = code_v[pl.ds(chunk * NB + b, 1), :]
         for layer in range(LAYERS):
             own_x = jnp.broadcast_to((code - float(layer * CX)).astype(BF16), (CX, BLK))
-            oh_v[chunk, pl.ds(layer * CX, CX), pl.ds(b * BLK, BLK)] = jnp.where(
+            oh_v[chunk, b, pl.ds(layer * CX, CX), :] = jnp.where(
                 own_x == iota_x, one16, zero16
             )
 
@@ -353,7 +353,7 @@
                 one_hot(chunk, b)
             wide = jnp.dot(
                 f16_v[...],
-                oh_v[chunk, :, first * BLK : (first + SUB) * BLK],
+                jnp.concatenate([oh_v[chunk, first + b] for b in range(SUB)], axis=1),
                 preferred_element_type=F32,
             )
             for b in range(SUB):
@@ -396,11 +396,14 @@
             hit = jnp.broadcast_to(y_v[pl.ds(p, 1), :].astype(BF16), (CY, BLK)) == iota_y16
             change = cr[p]
             for c in range(NC):
-                lhs_v[pl.ds(c * CY, CY), pl.ds(b * BLK, BLK)] = jnp.where(
+                lhs_v[b, pl.ds(c * CY, CY), :] = jnp.where(
                     hit, jnp.broadcast_to(change[c : c + 1], (CY, BLK)), zero16[:CY]
                 )
         added = lax.dot_general(
-            lhs_v[...], oh_v[chunk], (((1,), (1,)), ((), ())), preferred_element_type=F32
+            jnp.concatenate([lhs_v[b] for b in range(NB)], axis=1),
+            jnp.concatenate([oh_v[chunk, b] for b in range(NB)], axis=1),
+            (((1,), (1,)), ((), ())),
+            preferred_element_type=F32,
         )
         for layer in range(LAYERS):
             rows = pl.ds(layer * NC * CY, NC * CY)
@@ -560,8 +563,8 @@
             pltpu.VMEM((FIELDS * CY, CX), F32),
             pltpu.VMEM((BLOCKS, BLK), F32),
             pltpu.VMEM((BLOCKS, BLK), F32),
-            pltpu.VMEM((CHUNKS, LAYERS * CX, NB * BLK), BF16),
-            pltpu.VMEM((NC * CY, NB * BLK), BF16),
+            pltpu.VMEM((CHUNKS, NB, LAYERS * CX, BLK), BF16),
+            pltpu.VMEM((NB, NC * CY, BLK), BF16),
             pltpu.VMEM((BLOCKS, NC, BLK), BF16),
             pltpu.VMEM((BLOCKS, NC, BLK), BF16),
             pltpu.VMEM((BLOCKS, NC, BLK), BF16),

time: 65.3 us -> 65.2 us (level)
  no operation moved by 1% of the time
where the time goes in v5:
time: 65.2 us; the launch traced here: 64.6 us
  Pallas kernels  61.6 us (94%)
  local copies, waits for them, and re-layouts  1.74 us (3%)
  between operations  1.29 us (2%)
    pallas_call x1, Pallas kernels, shards(): pl.pallas_call(kernel, out_shape=(pltpu.VMEM((FIELDS * CY, CX), F32), plt...  61.6 us
    unnamed x2, local copies, waits for them, and re-layouts  1.74 us

profile of v5, /device:TPU:1, one launch (start us, length us, event | category | flops | bytes accessed | tf_op | source)
XLA Modules:
  0.0 64.6 jit_solution(9758276310350491441)
XLA Ops:
  1.3 61.6 %shard_map.122 = (f32[3072,128]{1,0:T(8,128)S(1)}, f32[8,8]{1,0:T(8,128)S(1)}) custom-call(f32[3072,128]{1,0:T(8,128)} %bitcast.11, f32[384,128]{1,0:T(8,128)} %bitcast.13, s32[64,128]{1,0:T(8,128)} %mask_h.1, bf16[6,8,8,64,128]{4,3,2,1,0:T(8,128)(2,1)} %diag_h.1, bf16[6,8,8,64,128]{4,3,2,1,0:T(8,128)(2,1)} %flux_h.1, s32[128,128]{1,0:T(8,128)} %bitcast.14, ...), custom_call_target="tpu_custom_call" | custom-call | tf_op jit(solution)/shard_map/pallas_call | solution.py:538
  62.9 1.1 %copy.15 = f32[6,8,64,128]{3,2,1,0:T(8,128)} copy(f32[6,8,64,128]{3,2,1,0:T(8,128)S(1)} %bitcast.8) | data formatting | bytes 3145728
  64.0 0.6 copy.16
